TPU v7x, 256 devices: a whole 4x4x8 slice. The times are simulated.
256 devices in a mesh: img: 128 (over z, x, y), rep: 2 (over core).
Axes of the slice: x: 4, y: 4, z: 8, core: 2. Of those that a mesh axis runs over, the one named last changes fastest.
Arguments:
- panels: float32 [256, 512, 128], P('img', 'rep'), may hold values from -6 to 6
- blocks: bfloat16 [6144, 512, 512], P('img', None, 'rep'), may hold values from -0.25 to 0.25
- pairs: int32 [6144, 2], P('img'), may hold values from 0 to 255, as said below
- counts: int32 [128], P('img'), may hold values from 12 to 48, as said below
Outputs:
- basis: float32 [256, 512, 128], P('img', 'rep')
Inputs may be any that keep to these rules, and one draw needn't show every extreme that they name: `pairs`: row d * 48 + s is slot s of index d of img: its first image is one of d * 2 to d * 2 + 1, its second image lies on one of the indices d + 1 to d + 8 modulo 128. At most 6 slots of one index name second images on one other index, and that many is reached. `counts`: some index of img has all 48 slots live.
All inputs are finite; a program needn't handle non-finite values.
Results may differ from a plain program's by a relative error of at most 0.0025.
The roundings to bfloat16 on the way count: a program that leaves them out, or rounds other values in their place, can miss the bound.
Values may be sent and summed in bfloat16 or wider, within the bound.
A program may use at most 128 MiB of HBM per device.

v0:
```python
import jax
import jax.numpy as jnp
from jax import lax
from jax.sharding import PartitionSpec as P

BAND = 8


def passed_along(value, axis, steps):
    count = lax.axis_size(axis)
    pairs = [(source, (source + steps) % count) for source in range(count)]
    return lax.ppermute(value, axis, pairs)


def shards(panels, blocks, pairs, counts):
    devices = lax.axis_size("img")
    own_index = lax.axis_index("img")
    img_dev = panels.shape[0]
    half_rows = panels.shape[1]
    univ_cols = panels.shape[2]
    pair_dev = blocks.shape[0]
    keypts = blocks.shape[1]
    band_width = BAND
    capacity = pair_dev // band_width
    buffer_rows = band_width * capacity
    rounded = panels.astype(jnp.bfloat16)
    own_full = lax.all_gather(rounded, "rep", axis=1, tiled=True)
    live_count = counts[0]
    slot_ids = jnp.arange(pair_dev)
    alive = slot_ids < live_count
    first_local = jnp.clip(pairs[:, 0] - own_index * img_dev, 0, img_dev - 1)
    peers = pairs[:, 1] // img_dev
    second_local = pairs[:, 1] - peers * img_dev
    offsets = (peers - own_index - 1) % devices
    peer_hits = ((offsets[:, None] == jnp.arange(band_width)[None, :]) & alive[:, None]).astype(
        jnp.int32
    )
    ranks = jnp.sum(jnp.cumsum(peer_hits, axis=0) * peer_hits, axis=1) - 1
    targets = jnp.where(alive, offsets * capacity + ranks, buffer_rows)
    slot_hits = (targets[:, None] == jnp.arange(buffer_rows)[None, :]).astype(jnp.int32)
    asking = (jnp.sum(slot_hits * (second_local + 1)[:, None], axis=0) - 1).reshape(
        band_width, capacity
    )
    incoming = jnp.stack(
        [passed_along(asking[step], "img", step + 1) for step in range(band_width)]
    )
    incoming_flat = incoming.reshape(buffer_rows)
    chosen_rows = rounded[jnp.clip(incoming_flat, 0, img_dev - 1)]
    outbound = jnp.where(
        (incoming_flat >= 0)[:, None, None], chosen_rows, jnp.zeros_like(chosen_rows)
    )
    outbound = outbound.reshape(band_width, capacity, half_rows, univ_cols)
    arrived = jnp.concatenate(
        [passed_along(outbound[step], "img", -(step + 1)) for step in range(band_width)], axis=0
    )
    second_panels = arrived[jnp.where(alive, targets, 0)]
    first_panels = own_full[first_local]
    group_width = 8

    def one_group(group, carry):
        forward, reverse = carry
        start = group * group_width
        block_rows = lax.dynamic_slice_in_dim(blocks, start, group_width, 0)
        far_rows = lax.dynamic_slice_in_dim(second_panels, start, group_width, 0)
        near_rows = lax.dynamic_slice_in_dim(first_panels, start, group_width, 0)
        alive_rows = lax.dynamic_slice_in_dim(alive, start, group_width, 0)
        owners = lax.dynamic_slice_in_dim(first_local, start, group_width, 0)
        products = jnp.einsum(
            "skh,shn->skn", block_rows, far_rows, preferred_element_type=jnp.float32
        )
        weights = ((owners[None, :] == jnp.arange(img_dev)[:, None]) & alive_rows[None, :]).astype(
            jnp.float32
        )
        forward = forward + jnp.sum(weights[:, :, None, None] * products[None], axis=1)
        turned = jnp.einsum(
            "skh,skn->shn", block_rows, near_rows, preferred_element_type=jnp.float32
        ).astype(jnp.bfloat16)
        reverse = lax.dynamic_update_slice_in_dim(reverse, turned, start, 0)
        return (forward, reverse)

    initial = (
        jnp.zeros((img_dev, keypts, univ_cols), jnp.float32),
        jnp.zeros((pair_dev, half_rows, univ_cols), jnp.bfloat16),
    )
    forward, reverse = lax.fori_loop(
        0, (live_count + group_width - 1) // group_width, one_group, initial
    )
    outgoing = (
        jnp.zeros((buffer_rows, half_rows, univ_cols), jnp.bfloat16)
        .at[targets]
        .set(reverse, mode="drop")
    )
    outgoing = outgoing.reshape(band_width, capacity, half_rows, univ_cols)
    received = jnp.concatenate(
        [passed_along(outgoing[step], "img", step + 1) for step in range(band_width)], axis=0
    )
    image_pick = (incoming_flat[None, :] == jnp.arange(img_dev)[:, None]).astype(jnp.bfloat16)
    returned_sum = jnp.einsum(
        "ir,rkn->ikn", image_pick, received, preferred_element_type=jnp.float32
    )
    forward_half = lax.psum_scatter(forward, "rep", scatter_dimension=1, tiled=True)
    field = panels + forward_half + returned_sum
    gram_local = jnp.einsum(
        "ikn,ikm->nm",
        field,
        field,
        precision=lax.Precision.HIGHEST,
        preferred_element_type=jnp.float32,
    )
    gram_matrix = lax.psum(gram_local, ("img", "rep"))
    gram_matrix = gram_matrix / (devices * img_dev * keypts)
    factor = jnp.linalg.cholesky(gram_matrix)
    stacked = field.reshape(img_dev * half_rows, univ_cols)
    basis = lax.linalg.triangular_solve(
        factor, stacked, left_side=False, lower=True, transpose_a=True
    )
    return basis.reshape(img_dev, half_rows, univ_cols)


def solution(mesh):
    in_specs = (P("img", "rep", None), P("img", None, "rep"), P("img", None), P("img"))
    out_specs = P("img", "rep", None)
    return jax.shard_map(shards, mesh=mesh, in_specs=in_specs, out_specs=out_specs, check_vma=False)
```

profile of v0, /device:TPU:1, one launch (start us, length us, event | category | flops | bytes accessed | tf_op | source)
XLA Modules:
  0.0 617.6 jit_solution(9998601148307010880)
XLA Ops:
  12.7 3.5 collective-permute-start.5
  40.2 6.3 %all_gather.3 = bf16[2,512,128]{2,1,0:T(8,128)(2,1)S(1)} all-gather(bf16[2,256,128]{2,1,0:T(8,128)(2,1)S(1)} %convert_element_type.19), channel_id=1, replica_groups=mesh['img'=128,'rep'=2] {'rep'}, dimensions={1}, use_global_device_ids=true | all-gather | bytes 393216 | tf_op jit(solution)/shard_map/all_gather | solution.py:27
  46.5 4.8 gather_fusion.2
  51.3 12.4 %collective-permute-start.12 = (bf16[6,256,128]{2,1,0:T(8,128)(2,1)}, bf16[6,256,128]{2,1,0:T(8,128)(2,1)S(1)}, u32[]{:S(2)}, u32[]{:S(2)}) collective-permute-start(bf16[6,256,128]{2,1,0:T(8,128)(2,1)} %get-tuple-element.98), channel_id=1, source_target_pairs={{0,246},{2,248},{4,250},{6,252},{8,254},{10,0},{12,2},{14,4},{16,6... | collective-permute-start | bytes 1179656 | tf_op jit(solution)/shard_map/ppermute | solution.py:12
  69.8 4.3 collective-permute-start.15
  75.1 14.9 %collective-permute-done.11 = bf16[6,256,128]{2,1,0:T(8,128)(2,1)} collective-permute-done((bf16[6,256,128]{2,1,0:T(8,128)(2,1)}, bf16[6,256,128]{2,1,0:T(8,128)(2,1)}, u32[]{:S(2)}, u32[]{:S(2)}) %collective-permute-start.11) | collective-permute-done | bytes 393248 | tf_op jit(solution)/shard_map/ppermute | solution.py:12
  91.7 6.6 %collective-permute-done.14 = bf16[6,256,128]{2,1,0:T(8,128)(2,1)S(1)} collective-permute-done((bf16[6,256,128]{2,1,0:T(8,128)(2,1)}, bf16[6,256,128]{2,1,0:T(8,128)(2,1)S(1)}, u32[]{:S(2)}, u32[]{:S(2)}) %collective-permute-start.14) | collective-permute-done | bytes 393248 | tf_op jit(solution)/shard_map/ppermute | solution.py:12
  98.3 10.3 %collective-permute-done.15 = bf16[6,256,128]{2,1,0:T(8,128)(2,1)S(1)} collective-permute-done((bf16[6,256,128]{2,1,0:T(8,128)(2,1)S(1)}, bf16[6,256,128]{2,1,0:T(8,128)(2,1)S(1)}, u32[]{:S(2)}, u32[]{:S(2)}) %collective-permute-start.15) | collective-permute-done | bytes 393248 | tf_op jit(solution)/shard_map/ppermute | solution.py:12
  114.0 39.1 %while.12 = (s32[]{:T(128)}, f32[2,512,128]{2,1,0:T(8,128)S(1)}, bf16[48,256,128]{2,1,0:T(8,128)(2,1)}, s32[]{:T(128)}, s32[48]{0:T(128)S(1)}, /*index=5*/pred[4...) while((s32[]{:T(128)}, f32[2,512,128]{2,1,0:T(8,128)S(1)}, ...), condition=%wide.region_5.6_spmd, body=%wide.region_3.5_spmd.sunk | while | flops 539230272 | bytes 12585899 | solution.py:85
  117.0 3.5 fusion.47
  123.5 3.5 fusion.47
  130.1 3.5 fusion.47
  136.6 3.5 fusion.47
  143.1 3.5 fusion.47
  149.6 3.5 fusion.47
  154.6 5.7 scatter_fusion
  168.3 16.0 %collective-permute-done.16 = bf16[6,256,128]{2,0,1:T(8,128)(2,1)} collective-permute-done((bf16[6,256,128]{2,0,1:T(8,128)(2,1)S(1)}, bf16[6,256,128]{2,0,1:T(8,128)(2,1)}, u32[]{:S(2)}, u32[]{:S(2)}) %collective-permute-start.16) | collective-permute-done | bytes 393248 | tf_op jit(solution)/shard_map/ppermute | solution.py:12
  185.3 28.6 %collective-permute-start.23 = (bf16[6,256,128]{2,0,1:T(8,128)(2,1)S(1)}, bf16[6,256,128]{2,0,1:T(8,128)(2,1)}, u32[]{:S(2)}, u32[]{:S(2)}) collective-permute-start(bf16[6,256,128]{2,0,1:T(8,128)(2,1)S(1)} %copy.97), channel_id=1, source_target_pairs={{0,16},{2,18},{4,20},{6,22},{8,24},{10,26},{12,28},{14,30},{16,32}... | collective-permute-start | bytes 1179656 | tf_op jit(solution)/shard_map/ppermute | solution.py:12
  218.5 6.6 %collective-permute-done.23 = bf16[6,256,128]{2,0,1:T(8,128)(2,1)} collective-permute-done((bf16[6,256,128]{2,0,1:T(8,128)(2,1)S(1)}, bf16[6,256,128]{2,0,1:T(8,128)(2,1)}, u32[]{:S(2)}, u32[]{:S(2)}) %collective-permute-start.23) | collective-permute-done | bytes 393248 | tf_op jit(solution)/shard_map/ppermute | solution.py:12
  225.0 39.1 %concatenate.7 = bf16[48,256,128]{2,0,1:T(8,128)(2,1)S(1)} concatenate(bf16[6,256,128]{2,0,1:T(8,128)(2,1)} %collective-permute-done.16, bf16[6,256,128]{2,0,1:T(8,128)(2,1)} %collective-permute-done.17, bf16[6,256,128]{2,0,1:T(8,128)(2,1)} %collective-permute-done.18, bf16[6,256,128]{2,0,1:T(8,128)(2,1)} %copy-done.2, bf16[6,256,128]{2,0,1:T(8,128)(2,1)} %copy-done.3, ...), dimensions={0} | concatenate | bytes 6291456 | tf_op jit(solution)/shard_map/concatenate | solution.py:94
  264.6 29.3 %all-reduce.6.cloned.1.call-done = f32[2,512,128]{2,0,1:T(2,128)} async-done(((f32[2,512,128]{2,0,1:T(2,128)}), f32[2,512,128]{2,0,1:T(2,128)}) %all-reduce.6.cloned.1.call-update) | async-done | bytes 524304
  297.3 286.4 %all-reduce.4.cloned.1.call-done = f32[128,128]{0,1:T(8,128)} async-done(((f32[128,128]{0,1:T(8,128)}), f32[128,128]{0,1:T(8,128)}) %all-reduce.4.cloned.1.call-update) | async-done | bytes 65552 | tf_op jit(solution)/shard_map/psum | solution.py:110
  585.5 11.7 %cholesky.16 = f32[128,128]{1,0:T(8,128)S(1)} custom-call(f32[128,128]{1,0:T(8,128)S(1)} %fusion.17), custom_call_target="Cholesky" | custom-call | tf_op jit(solution)/shard_map/jit(cholesky)/cholesky | solution.py:112
  598.5 9.8 %custom-call.6 = f32[1,128,128]{1,2,0:T(8,128)S(1)} custom-call(f32[1,128,128]{2,1,0:T(8,128)S(1)} %fusion.14), custom_call_target="InvertDiagBlocksLowerTriangular" | custom-call | tf_op jit(solution)/shard_map/triangular_solve | solution.py:114
  (157 shorter events, 84.8 us)
Async XLA Ops:
  6.5 287.4 %all-reduce.6.cloned.1.call-start = ((), (), s32[]{:S(2)}) async-start(), calls=%async_computation.1 | async-start | bytes 1048576
  9.6 13.3 %collective-permute-start.4 = (s32[6]{0:T(128)S(1)}, s32[6]{0:T(128)S(1)}, u32[]{:S(2)}, u32[]{:S(2)}) collective-permute-start(s32[6]{0:T(128)S(1)} %get-tuple-element.108), channel_id=1, source_target_pairs={{0,10},{2,12},{4,14},{6,16},{8,18},{10,20},{12,22},{14,24},{16,26}... | collective-permute-start | bytes 80 | tf_op jit(solution)/shard_map/ppermute | solution.py:12
  12.7 11.7 %collective-permute-start.5 = (s32[6]{0:T(128)S(1)}, s32[6]{0:T(128)S(1)}, u32[]{:S(2)}, u32[]{:S(2)}) collective-permute-start(s32[6]{0:T(128)S(1)} %get-tuple-element.107), channel_id=1, source_target_pairs={{0,12},{2,14},{4,16},{6,18},{8,20},{10,22},{12,24},{14,26},{16,28}... | collective-permute-start | bytes 80 | tf_op jit(solution)/shard_map/ppermute | solution.py:12
  16.2 10.2 %collective-permute-start.6 = (s32[6]{0:T(128)S(1)}, s32[6]{0:T(128)S(1)}, u32[]{:S(2)}, u32[]{:S(2)}) collective-permute-start(s32[6]{0:T(128)S(1)} %get-tuple-element.106), channel_id=1, source_target_pairs={{0,14},{2,16},{4,18},{6,20},{8,22},{10,24},{12,26},{14,28},{16,30}... | collective-permute-start | bytes 80 | tf_op jit(solution)/shard_map/ppermute | solution.py:12
  19.2 8.5 %collective-permute-start.7 = (s32[6]{0:T(128)S(1)}, s32[6]{0:T(128)S(1)}, u32[]{:S(2)}, u32[]{:S(2)}) collective-permute-start(s32[6]{0:T(128)S(1)} %get-tuple-element.105), channel_id=1, source_target_pairs={{0,16},{2,18},{4,20},{6,22},{8,24},{10,26},{12,28},{14,30},{16,32}... | collective-permute-start | bytes 80 | tf_op jit(solution)/shard_map/ppermute | solution.py:12
  21.9 7.8 %collective-permute-start = (s32[6]{0:T(128)S(1)}, s32[6]{0:T(128)S(1)}, u32[]{:S(2)}, u32[]{:S(2)}) collective-permute-start(s32[6]{0:T(128)S(1)} %get-tuple-element.112), channel_id=1, source_target_pairs={{0,2},{2,4},{4,6},{6,8},{8,10},{10,12},{12,14},{14,16},{16,18},{18... | collective-permute-start | bytes 80 | tf_op jit(solution)/shard_map/ppermute | solution.py:12
  22.9 8.2 %collective-permute-start.1 = (s32[6]{0:T(128)S(1)}, s32[6]{0:T(128)S(1)}, u32[]{:S(2)}, u32[]{:S(2)}) collective-permute-start(s32[6]{0:T(128)S(1)} %get-tuple-element.111), channel_id=1, source_target_pairs={{0,4},{2,6},{4,8},{6,10},{8,12},{10,14},{12,16},{14,18},{16,20},{1... | collective-permute-start | bytes 80 | tf_op jit(solution)/shard_map/ppermute | solution.py:12
  35.3 28.4 %collective-permute-start.8 = (bf16[6,256,128]{2,1,0:T(8,128)(2,1)S(1)}, bf16[6,256,128]{2,1,0:T(8,128)(2,1)S(1)}, u32[]{:S(2)}, u32[]{:S(2)}) collective-permute-start(bf16[6,256,128]{2,1,0:T(8,128)(2,1)S(1)} %get-tuple-element.102), channel_id=1, source_target_pairs={{0,254},{2,0},{4,2},{6,4},{8,6},{10,8},{12,10},{14,12},{16,14},{18... | collective-permute-start | bytes 1179656 | tf_op jit(solution)/shard_map/ppermute | solution.py:12
  37.0 30.2 %collective-permute-start.9 = (bf16[6,256,128]{2,1,0:T(8,128)(2,1)}, bf16[6,256,128]{2,1,0:T(8,128)(2,1)}, u32[]{:S(2)}, u32[]{:S(2)}) collective-permute-start(bf16[6,256,128]{2,1,0:T(8,128)(2,1)} %get-tuple-element.101), channel_id=1, source_target_pairs={{0,252},{2,254},{4,0},{6,2},{8,4},{10,6},{12,8},{14,10},{16,12},{1... | collective-permute-start | bytes 1179656 | tf_op jit(solution)/shard_map/ppermute | solution.py:12
  39.3 30.5 %collective-permute-start.10 = (bf16[6,256,128]{2,1,0:T(8,128)(2,1)}, bf16[6,256,128]{2,1,0:T(8,128)(2,1)}, u32[]{:S(2)}, u32[]{:S(2)}) collective-permute-start(bf16[6,256,128]{2,1,0:T(8,128)(2,1)} %get-tuple-element.100), channel_id=1, source_target_pairs={{0,250},{2,252},{4,254},{6,0},{8,2},{10,4},{12,6},{14,8},{16,10},{... | collective-permute-start | bytes 1179656 | tf_op jit(solution)/shard_map/ppermute | solution.py:12
  40.1 49.9 %collective-permute-start.11 = (bf16[6,256,128]{2,1,0:T(8,128)(2,1)}, bf16[6,256,128]{2,1,0:T(8,128)(2,1)}, u32[]{:S(2)}, u32[]{:S(2)}) collective-permute-start(bf16[6,256,128]{2,1,0:T(8,128)(2,1)} %get-tuple-element.99), channel_id=1, source_target_pairs={{0,248},{2,250},{4,252},{6,254},{8,0},{10,2},{12,4},{14,6},{16,8},... | collective-permute-start | bytes 1179656 | tf_op jit(solution)/shard_map/ppermute | solution.py:12
  51.3 39.8 %collective-permute-start.12 = (bf16[6,256,128]{2,1,0:T(8,128)(2,1)}, bf16[6,256,128]{2,1,0:T(8,128)(2,1)S(1)}, u32[]{:S(2)}, u32[]{:S(2)}) collective-permute-start(bf16[6,256,128]{2,1,0:T(8,128)(2,1)} %get-tuple-element.98), channel_id=1, source_target_pairs={{0,246},{2,248},{4,250},{6,252},{8,254},{10,0},{12,2},{14,4},{16,6... | collective-permute-start | bytes 1179656 | tf_op jit(solution)/shard_map/ppermute | solution.py:12
  64.4 27.3 %collective-permute-start.13 = (bf16[6,256,128]{2,1,0:T(8,128)(2,1)}, bf16[6,256,128]{2,1,0:T(8,128)(2,1)S(1)}, u32[]{:S(2)}, u32[]{:S(2)}) collective-permute-start(bf16[6,256,128]{2,1,0:T(8,128)(2,1)} %get-tuple-element.97), channel_id=1, source_target_pairs={{0,244},{2,246},{4,248},{6,250},{8,252},{10,254},{12,0},{14,2},{16... | collective-permute-start | bytes 1179656 | tf_op jit(solution)/shard_map/ppermute | solution.py:12
  67.2 31.1 %collective-permute-start.14 = (bf16[6,256,128]{2,1,0:T(8,128)(2,1)}, bf16[6,256,128]{2,1,0:T(8,128)(2,1)S(1)}, u32[]{:S(2)}, u32[]{:S(2)}) collective-permute-start(bf16[6,256,128]{2,1,0:T(8,128)(2,1)} %get-tuple-element.96), channel_id=1, source_target_pairs={{0,242},{2,244},{4,246},{6,248},{8,250},{10,252},{12,254},{14,0},{... | collective-permute-start | bytes 1179656 | tf_op jit(solution)/shard_map/ppermute | solution.py:12
  69.8 38.9 %collective-permute-start.15 = (bf16[6,256,128]{2,1,0:T(8,128)(2,1)S(1)}, bf16[6,256,128]{2,1,0:T(8,128)(2,1)S(1)}, u32[]{:S(2)}, u32[]{:S(2)}) collective-permute-start(bf16[6,256,128]{2,1,0:T(8,128)(2,1)S(1)} %get-tuple-element.95), channel_id=1, source_target_pairs={{0,240},{2,242},{4,244},{6,246},{8,248},{10,250},{12,252},{14,254}... | collective-permute-start | bytes 1179656 | tf_op jit(solution)/shard_map/ppermute | solution.py:12
  161.0 23.3 %collective-permute-start.16 = (bf16[6,256,128]{2,0,1:T(8,128)(2,1)S(1)}, bf16[6,256,128]{2,0,1:T(8,128)(2,1)}, u32[]{:S(2)}, u32[]{:S(2)}) collective-permute-start(bf16[6,256,128]{2,0,1:T(8,128)(2,1)S(1)} %copy.90), channel_id=1, source_target_pairs={{0,2},{2,4},{4,6},{6,8},{8,10},{10,12},{12,14},{14,16},{16,18},{18... | collective-permute-start | bytes 1179656 | tf_op jit(solution)/shard_map/ppermute | solution.py:12
  161.4 24.0 %collective-permute-start.17 = (bf16[6,256,128]{2,0,1:T(8,128)(2,1)S(1)}, bf16[6,256,128]{2,0,1:T(8,128)(2,1)}, u32[]{:S(2)}, u32[]{:S(2)}) collective-permute-start(bf16[6,256,128]{2,0,1:T(8,128)(2,1)S(1)} %copy.91), channel_id=1, source_target_pairs={{0,4},{2,6},{4,8},{6,10},{8,12},{10,14},{12,16},{14,18},{16,20},{1... | collective-permute-start | bytes 1179656 | tf_op jit(solution)/shard_map/ppermute | solution.py:12
  161.8 23.6 %collective-permute-start.18 = (bf16[6,256,128]{2,0,1:T(8,128)(2,1)S(1)}, bf16[6,256,128]{2,0,1:T(8,128)(2,1)}, u32[]{:S(2)}, u32[]{:S(2)}) collective-permute-start(bf16[6,256,128]{2,0,1:T(8,128)(2,1)S(1)} %copy.92), channel_id=1, source_target_pairs={{0,6},{2,8},{4,10},{6,12},{8,14},{10,16},{12,18},{14,20},{16,22},{... | collective-permute-start | bytes 1179656 | tf_op jit(solution)/shard_map/ppermute | solution.py:12
  162.1 54.3 %collective-permute-start.19 = (bf16[6,256,128]{2,0,1:T(8,128)(2,1)S(1)}, bf16[6,256,128]{2,0,1:T(8,128)(2,1)S(1)}, u32[]{:S(2)}, u32[]{:S(2)}) collective-permute-start(bf16[6,256,128]{2,0,1:T(8,128)(2,1)S(1)} %copy.93), channel_id=1, source_target_pairs={{0,8},{2,10},{4,12},{6,14},{8,16},{10,18},{12,20},{14,22},{16,24},... | collective-permute-start | bytes 1179656 | tf_op jit(solution)/shard_map/ppermute | solution.py:12
  163.8 52.7 %collective-permute-start.20 = (bf16[6,256,128]{2,0,1:T(8,128)(2,1)}, bf16[6,256,128]{2,0,1:T(8,128)(2,1)S(1)}, u32[]{:S(2)}, u32[]{:S(2)}) collective-permute-start(bf16[6,256,128]{2,0,1:T(8,128)(2,1)} %copy.94), channel_id=1, source_target_pairs={{0,10},{2,12},{4,14},{6,16},{8,18},{10,20},{12,22},{14,24},{16,26}... | collective-permute-start | bytes 1179656 | tf_op jit(solution)/shard_map/ppermute | solution.py:12
  184.3 32.2 %collective-permute-start.21 = (bf16[6,256,128]{2,0,1:T(8,128)(2,1)}, bf16[6,256,128]{2,0,1:T(8,128)(2,1)S(1)}, u32[]{:S(2)}, u32[]{:S(2)}) collective-permute-start(bf16[6,256,128]{2,0,1:T(8,128)(2,1)} %copy.95), channel_id=1, source_target_pairs={{0,12},{2,14},{4,16},{6,18},{8,20},{10,22},{12,24},{14,26},{16,28}... | collective-permute-start | bytes 1179656 | tf_op jit(solution)/shard_map/ppermute | solution.py:12
  185.3 31.2 %collective-permute-start.22 = (bf16[6,256,128]{2,0,1:T(8,128)(2,1)}, bf16[6,256,128]{2,0,1:T(8,128)(2,1)S(1)}, u32[]{:S(2)}, u32[]{:S(2)}) collective-permute-start(bf16[6,256,128]{2,0,1:T(8,128)(2,1)} %copy.96), channel_id=1, source_target_pairs={{0,14},{2,16},{4,18},{6,20},{8,22},{10,24},{12,26},{14,28},{16,30}... | collective-permute-start | bytes 1179656 | tf_op jit(solution)/shard_map/ppermute | solution.py:12
  185.3 39.7 %collective-permute-start.23 = (bf16[6,256,128]{2,0,1:T(8,128)(2,1)S(1)}, bf16[6,256,128]{2,0,1:T(8,128)(2,1)}, u32[]{:S(2)}, u32[]{:S(2)}) collective-permute-start(bf16[6,256,128]{2,0,1:T(8,128)(2,1)S(1)} %copy.97), channel_id=1, source_target_pairs={{0,16},{2,18},{4,20},{6,22},{8,24},{10,26},{12,28},{14,30},{16,32}... | collective-permute-start | bytes 1179656 | tf_op jit(solution)/shard_map/ppermute | solution.py:12
  215.2 368.5 %all-reduce.4.cloned.1.call-start = ((), (), s32[]{:S(2)}) async-start(), calls=%async_computation | async-start | bytes 131072 | tf_op jit(solution)/shard_map/psum | solution.py:110
  (13 other events, 133.9 us)
Sparse Core Ops, SparseCore 0:
  215.3 78.6 all-reduce.5
  299.5 284.1 all-reduce.3
where the time goes:
time: 629 us; the launch traced here: 618 us
  waiting for transfers between devices  376 us (60%)
  local copies, waits for them, and re-layouts  74.9 us (12%)
  starting transfers between devices  72.9 us (12%)
  matrix products  39.9 us (6%)
  other arithmetic  31.7 us (5%)
  between operations  15.5 us (2%)
    psum x1, waiting for transfers between devices, shards(): gram_matrix = lax.psum(gram_local, ('img', 'rep'))  286 us
    ppermute x24, starting transfers between devices, passed_along(): return lax.ppermute(value, axis, pairs)  72.9 us
    ppermute x24, waiting for transfers between devices, passed_along(): return lax.ppermute(value, axis, pairs)  60.5 us
    concatenate x1, local copies, waits for them, and re-layouts, shards(): jnp.concatenate([passed_along(outgoing[step], 'img', step + 1) for step i...  39.1 us
    unnamed x3, waiting for transfers between devices  29.4 us
    dot_general x6, matrix products, one_group(): jnp.einsum('skh,skn->shn', block_rows, near_rows, preferred_element_type=...  20.8 us
    dot_general x6, matrix products, one_group(): jnp.einsum('skh,shn->skn', block_rows, far_rows, preferred_element_type=j...  14.2 us
    unnamed x39, local copies, waits for them, and re-layouts  14 us
  transfers between devices with their start and end apart: 26, of which 13 were waited for; matrix products, arithmetic and copies ran while one was open for 9% of the time, Pallas kernels for 0%

commit v1 on v0

v1 whole, which is shorter than its diff:
```python
import functools

import jax
import jax.numpy as jnp
from jax import lax
from jax.experimental import pallas as pl
from jax.experimental.pallas import tpu as pltpu
from jax.sharding import PartitionSpec as P

MESH = pl.DeviceIdType.MESH
BAND = 8
PLANE = 16
CHUNKS = 8
VMEM_LIMIT = 60 * 1024 * 1024


def remote(src, dst, send_sem, recv_sem, img, rep):
    return pltpu.make_async_remote_copy(
        src_ref=src,
        dst_ref=dst,
        send_sem=send_sem,
        recv_sem=recv_sem,
        device_id=(img, rep),
        device_id_type=MESH,
    )


def pair_tables(pairs, counts):
    slots = pairs.shape[0]
    capacity = slots // BAND
    devices = lax.axis_size("img")
    own = lax.axis_index("img")
    ids = jnp.arange(slots, dtype=jnp.int32)
    alive = ids < counts[0]
    first = pairs[:, 0] & 1
    second = pairs[:, 1] & 1
    offset = (pairs[:, 1] // 2 - own - 1) % devices
    same = (offset[:, None] == offset[None, :]) & (ids[None, :] < ids[:, None])
    rank = jnp.sum((same & alive[None, :]).astype(jnp.int32), axis=1)
    target = jnp.where(alive, offset * capacity + rank, slots)
    near_0 = jnp.where(second == 0, first, 2)
    near_1 = jnp.where(second == 1, first, 2)
    code = ids * 16 + near_0 * 4 + near_1
    hit = target[None, :] == ids[:, None]
    empty = 2 * 4 + 2
    placed = empty + jnp.sum(jnp.where(hit, code - empty, 0), axis=1)
    far = offset * 2 + second
    far_0 = jnp.where(alive & (first == 0), far, 2 * BAND)
    far_1 = jnp.where(alive & (first == 1), far, 2 * BAND)
    return jnp.stack([placed // 16, (placed // 4) % 4, placed % 4, far_0, far_1])


def field_kernel(
    table,
    panels,
    rounded,
    blocks_hbm,
    field,
    gram,
    blocks,
    far,
    near_other,
    near,
    turned,
    returned,
    part,
    part_other,
    load_sem,
    far_send,
    far_recv,
    near_send,
    near_recv,
    back_send,
    back_recv,
    part_send,
    part_recv,
):
    me = lax.axis_index("img")
    rep = lax.axis_index("rep")
    devices = lax.axis_size("img")
    slots, keypts, half = blocks.shape
    univ = panels.shape[2]
    capacity = slots // BAND
    step = slots // CHUNKS

    def load(chunk):
        rows = pl.ds(chunk * step, step)
        return pltpu.make_async_copy(blocks_hbm.at[rows], blocks.at[rows], load_sem.at[chunk])

    for chunk in range(CHUNKS):
        load(chunk).start()

    barrier = pltpu.get_barrier_semaphore()

    def greet(k, _):
        up = (me + k + 1) % devices
        down = (me + devices - k - 1) % devices
        pl.semaphore_signal(barrier, inc=1, device_id=(up, rep), device_id_type=MESH)
        pl.semaphore_signal(barrier, inc=1, device_id=(down, rep), device_id_type=MESH)
        return 0

    lax.fori_loop(0, BAND, greet, 0)
    pl.semaphore_signal(barrier, inc=1, device_id=(me, 1 - rep), device_id_type=MESH)
    pl.semaphore_wait(barrier, 2 * BAND + 1)

    near_copy = remote(rounded, near_other, near_send, near_recv, me, 1 - rep)
    near_copy.start()

    def far_copy(k):
        down = (me + devices - k - 1) % devices
        return remote(
            rounded, far.at[pl.ds(2 * k, 2)], far_send.at[k], far_recv.at[k], down, rep
        )

    def start_far(t, _):
        far_copy(BAND - 1 - t).start()
        return 0

    lax.fori_loop(0, BAND, start_far, 0)
    far[2 * BAND] = jnp.zeros((half, univ), far.dtype)
    near[2] = jnp.zeros((univ, keypts), near.dtype)
    here = pl.ds(pl.multiple_of(rep * half, half), half)
    there = pl.ds(pl.multiple_of((1 - rep) * half, half), half)
    for image in range(2):
        near[image, :, here] = panels[image].T.astype(near.dtype)
    near_copy.wait()
    for image in range(2):
        near[image, :, there] = near_other[image].astype(jnp.float32).T.astype(near.dtype)
    for chunk in range(CHUNKS):
        load(chunk).wait()

    def back_copy(k):
        up = (me + k + 1) % devices
        return remote(turned.at[k], returned.at[k], back_send.at[k], back_recv.at[k], up, rep)

    def reverse(t, _):
        k = BAND - 1 - t
        total = jnp.zeros((2 * univ, half), jnp.float32)
        for r in range(capacity):
            q = k * capacity + r
            block = blocks[table[0, q]]
            rows = jnp.concatenate([near[table[1, q]], near[table[2, q]]], axis=0)
            product = jnp.dot(rows, block, preferred_element_type=jnp.float32)
            total = total + product.astype(jnp.bfloat16).astype(jnp.float32)
        for image in range(2):
            own = total[image * univ : (image + 1) * univ]
            turned[k, image] = own.T.astype(turned.dtype)
        back_copy(k).start()
        return 0

    lax.fori_loop(0, BAND, reverse, 0)

    def wait_far(k, _):
        far_copy(k).wait_recv()
        return 0

    lax.fori_loop(0, BAND, wait_far, 0)

    group = 4

    def forward(rows, out):
        out[...] = jnp.zeros_like(out)

        def one(g, _):
            left = []
            right = []
            for r in range(group):
                s = g * group + r
                left.append(blocks[s, rows, :])
                right.append(jnp.concatenate([far[table[3, s]], far[table[4, s]]], axis=1))
            out[...] += jnp.dot(
                jnp.concatenate(left, axis=1),
                jnp.concatenate(right, axis=0),
                preferred_element_type=jnp.float32,
            )
            return 0

        lax.fori_loop(0, slots // group, one, 0)

    part_copy = remote(part.at[0], part_other, part_send, part_recv, me, 1 - rep)
    forward(there, part.at[0])
    part_copy.start()
    forward(here, part.at[1])
    part_copy.wait_recv()

    def wait_back(k, _):
        back_copy(k).wait_recv()
        return 0

    lax.fori_loop(0, BAND, wait_back, 0)

    total = jnp.zeros((univ, univ), jnp.float32)
    for image in range(2):
        columns = pl.ds(image * univ, univ)
        value = panels[image] + part[1, :, columns] + part_other[:, columns]
        for k in range(BAND):
            value = value + returned[k, image].astype(jnp.float32)
        field[image] = value
        total = total + lax.dot_general(
            value,
            value,
            (((0,), (0,)), ((), ())),
            precision=lax.Precision.HIGHEST,
            preferred_element_type=jnp.float32,
        )
    for r in range(gram.shape[0]):
        gram[r] = total[r * gram.shape[1] : (r + 1) * gram.shape[1]]


    def wait_sends(k, _):
        far_copy(k).wait_send()
        back_copy(k).wait_send()
        return 0

    lax.fori_loop(0, BAND, wait_sends, 0)
    part_copy.wait_send()


def field_and_gram(table, panels, rounded, blocks):
    slots, keypts, half = blocks.shape
    univ = panels.shape[2]
    pieces = 2 * PLANE
    dma = pltpu.SemaphoreType.DMA
    return pl.pallas_call(
        field_kernel,
        out_shape=(
            jax.ShapeDtypeStruct(panels.shape, jnp.float32),
            jax.ShapeDtypeStruct((pieces, univ // pieces, univ), jnp.float32),
        ),
        in_specs=[
            pl.BlockSpec(memory_space=pltpu.SMEM),
            pl.BlockSpec(memory_space=pltpu.VMEM),
            pl.BlockSpec(memory_space=pltpu.VMEM),
            pl.BlockSpec(memory_space=pl.ANY),
        ],
        out_specs=(
            pl.BlockSpec(memory_space=pltpu.VMEM),
            pl.BlockSpec(memory_space=pltpu.VMEM),
        ),
        scratch_shapes=[
            pltpu.VMEM((slots, keypts, half), jnp.bfloat16),
            pltpu.VMEM((2 * BAND + 1, half, univ), jnp.bfloat16),
            pltpu.VMEM((2, half, univ), jnp.bfloat16),
            pltpu.VMEM((3, univ, keypts), jnp.bfloat16),
            pltpu.VMEM((BAND, 2, half, univ), jnp.bfloat16),
            pltpu.VMEM((BAND, 2, half, univ), jnp.bfloat16),
            pltpu.VMEM((2, half, 2 * univ), jnp.float32),
            pltpu.VMEM((half, 2 * univ), jnp.float32),
            dma((CHUNKS,)),
            dma((BAND,)),
            dma((BAND,)),
            dma,
            dma,
            dma((BAND,)),
            dma((BAND,)),
            dma,
            dma,
        ],
        compiler_params=pltpu.CompilerParams(
            collective_id=0, has_side_effects=True, vmem_limit_bytes=VMEM_LIMIT
        ),
        name="field",
    )(table, panels, rounded, blocks)


def sum_kernel(gram, out, parts, plane_sums, pieces, s1, r1, s2, r2, s3, r3):
    me = lax.axis_index("img")
    rep = lax.axis_index("rep")
    devices = lax.axis_size("img")
    levels = devices // PLANE
    size = 2 * PLANE
    level = me // PLANE
    rank = (me % PLANE) * 2 + rep
    base = level * PLANE

    def in_plane(t):
        other = (rank + t) % size
        return other, base + other // 2, other % 2

    def over_levels(t):
        return ((level + t) % levels) * PLANE + me % PLANE

    barrier = pltpu.get_barrier_semaphore()

    def greet_plane(t, _):
        _, img, core = in_plane(t)
        pl.semaphore_signal(barrier, inc=1, device_id=(img, core), device_id_type=MESH)
        return 0

    def greet_level(t, _):
        pl.semaphore_signal(
            barrier, inc=1, device_id=(over_levels(t), rep), device_id_type=MESH
        )
        return 0

    lax.fori_loop(1, levels, greet_level, 0)
    lax.fori_loop(1, size, greet_plane, 0)
    pl.semaphore_wait(barrier, size - 1 + levels - 1)

    def scatter(t):
        other, img, core = in_plane(t)
        return remote(gram.at[other], parts.at[t - 1], s1.at[t - 1], r1.at[t - 1], img, core)

    def across(t):
        return remote(
            plane_sums.at[level],
            plane_sums.at[level],
            s2.at[t - 1],
            r2.at[t - 1],
            over_levels(t),
            rep,
        )

    def across_in(t):
        from_level = (level + levels - t) % levels
        return remote(
            plane_sums.at[from_level],
            plane_sums.at[from_level],
            s2.at[t - 1],
            r2.at[t - 1],
            over_levels(t),
            rep,
        )

    def gather(t):
        _, img, core = in_plane(t)
        return remote(pieces.at[rank], pieces.at[rank], s3.at[t - 1], r3.at[t - 1], img, core)

    def gather_in(t):
        from_rank = (rank + size - t) % size
        _, img, core = in_plane(t)
        return remote(
            pieces.at[from_rank], pieces.at[from_rank], s3.at[t - 1], r3.at[t - 1], img, core
        )

    def each(first, last, act):
        def body(t, _):
            act(t)
            return 0

        lax.fori_loop(first, last, body, 0)

    each(1, size, lambda t: scatter(t).start())
    each(1, size, lambda t: scatter(t).wait_recv())
    total = gram[rank]
    for t in range(size - 1):
        total = total + parts[t]
    plane_sums[level] = total
    each(1, levels, lambda t: across(t).start())
    each(1, levels, lambda t: across_in(t).wait_recv())
    total = plane_sums[0]
    for t in range(1, levels):
        total = total + plane_sums[t]
    pieces[rank] = total
    each(1, size, lambda t: gather(t).start())
    each(1, size, lambda t: gather_in(t).wait_recv())
    width = gram.shape[1]
    for r in range(size):
        out[r * width : (r + 1) * width] = pieces[r]
    each(1, size, lambda t: scatter(t).wait_send())
    each(1, levels, lambda t: across(t).wait_send())
    each(1, size, lambda t: gather(t).wait_send())


def summed_gram(gram):
    size, width, univ = gram.shape
    levels = lax.axis_size("img") // PLANE
    dma = pltpu.SemaphoreType.DMA
    return pl.pallas_call(
        sum_kernel,
        out_shape=jax.ShapeDtypeStruct((size * width, univ), jnp.float32),
        in_specs=[pl.BlockSpec(memory_space=pltpu.VMEM)],
        out_specs=pl.BlockSpec(memory_space=pltpu.VMEM),
        scratch_shapes=[
            pltpu.VMEM((size - 1, width, univ), jnp.float32),
            pltpu.VMEM((levels, width, univ), jnp.float32),
            pltpu.VMEM((size, width, univ), jnp.float32),
            dma((size - 1,)),
            dma((size - 1,)),
            dma((levels - 1,)),
            dma((levels - 1,)),
            dma((size - 1,)),
            dma((size - 1,)),
        ],
        compiler_params=pltpu.CompilerParams(collective_id=1, has_side_effects=True),
        name="sum_gram",
    )(gram)


def basis_kernel(scale, gram, field, basis):
    univ = gram.shape[0]
    left = gram[...] * scale
    rows = lax.broadcasted_iota(jnp.int32, (univ, univ), 0)
    columns = lax.broadcasted_iota(jnp.int32, (univ, univ), 1)
    unit = (rows == columns).astype(jnp.float32)
    right = unit
    diagonal = jnp.zeros((univ, univ), jnp.float32)
    for j in range(univ):
        top = (j // 8) * 8
        low = left[top:]
        low_right = right[top:]
        row = low[j - top : j - top + 1]
        row_right = low_right[j - top : j - top + 1]
        pivot = row[:, j : j + 1]
        inverse = 1.0 / pivot
        below = rows[top:] > j
        factor = jnp.where(below, low[:, j : j + 1] * inverse, 0.0)
        diagonal = jnp.where(rows == j, lax.rsqrt(pivot), diagonal)
        low = low - factor * row
        low_right = low_right - factor * row_right
        left = jnp.concatenate([left[:top], low], axis=0) if top else low
        right = jnp.concatenate([right[:top], low_right], axis=0) if top else low_right
    inverse_factor = right * diagonal
    for image in range(field.shape[0]):
        basis[image] = lax.dot_general(
            field[image],
            inverse_factor,
            (((1,), (1,)), ((), ())),
            precision=lax.Precision.HIGHEST,
            preferred_element_type=jnp.float32,
        )


def shards(panels, blocks, pairs, counts):
    table = pair_tables(pairs, counts)
    rounded = panels.astype(jnp.bfloat16)
    field, gram = field_and_gram(table, panels, rounded, blocks)
    gram = summed_gram(gram)
    rows = lax.axis_size("img") * panels.shape[0] * lax.axis_size("rep") * panels.shape[1]
    return pl.pallas_call(
        functools.partial(basis_kernel, 1.0 / rows),
        out_shape=jax.ShapeDtypeStruct(panels.shape, jnp.float32),
        in_specs=[pl.BlockSpec(memory_space=pltpu.VMEM)] * 2,
        out_specs=pl.BlockSpec(memory_space=pltpu.VMEM),
        name="basis",
    )(gram, field)


def solution(mesh):
    in_specs = (P("img", "rep", None), P("img", None, "rep"), P("img", None), P("img"))
    out_specs = P("img", "rep", None)
    return jax.shard_map(shards, mesh=mesh, in_specs=in_specs, out_specs=out_specs, check_vma=False)
```

time: 629 us -> 96.5 us (0.15); the launches traced: 618 us -> 96.2 us
  waiting for transfers between devices: 376 us -> 0 us
  Pallas kernels: 0 us -> 90 us
  local copies, waits for them, and re-layouts: 74.9 us -> 0.61 us
  starting transfers between devices: 72.9 us -> 0 us
  matrix products: 39.9 us -> 0 us
  other arithmetic: 31.7 us -> 4.87 us
  between operations: 15.5 us -> 0.68 us
    psum x1 -> x0, waiting for transfers between devices: 286 us -> none  [shards(): gram_matrix = lax.psum(gram_local, ('img', 'rep'))]
    pallas_call x0 -> x3, Pallas kernels: none -> 90 us  [the longest x1 43 us: field_and_gram(): pl.pallas_call(field_kernel, out_shape=(jax.ShapeDtypeStruct(panels.shape...]
    ppermute x24 -> x0, starting transfers between devices: 72.9 us -> none  [passed_along(): return lax.ppermute(value, axis, pairs)]
    ppermute x24 -> x0, waiting for transfers between devices: 60.5 us -> none  [passed_along(): return lax.ppermute(value, axis, pairs)]
    concatenate x2 -> x0, local copies, waits for them, and re-layouts: 39.1 us -> none  [the longest x1 39.1 us: shards(): jnp.concatenate([passed_along(outgoing[step], 'img', step + 1) for step i...]
    dot_general x14 -> x0, matrix products: 37.9 us -> none  [the longest x6 20.8 us: one_group(): jnp.einsum('skh,skn->shn', block_rows, near_rows, preferred_element_type=...]
    unnamed x3 -> x0, waiting for transfers between devices: 29.4 us -> none
    another operation x6 -> x0, other arithmetic: 22.9 us -> none  [the longest x3 12.4 us: shards(): factor = jnp.linalg.cholesky(gram_matrix)]
  transfers between devices with their start and end apart: 26 -> 0, of which waited for: 13 -> 0; matrix products, arithmetic and copies ran while one was open for 9% -> 0% of each run, Pallas kernels for 0% -> 0%
where the time goes in v1:
time: 96.5 us; the launch traced here: 96.2 us
  Pallas kernels  90 us (93%)
  other arithmetic  4.87 us (5%)
    pallas_call x1, Pallas kernels, field_and_gram(): pl.pallas_call(field_kernel, out_shape=(jax.ShapeDtypeStruct(panels.shape...  43 us
    pallas_call x1, Pallas kernels, summed_gram(): pl.pallas_call(sum_kernel, out_shape=jax.ShapeDtypeStruct((size * width,...  34.2 us
    pallas_call x1, Pallas kernels, shards(): pl.pallas_call(functools.partial(basis_kernel, 1.0 / rows), out_shape=jax...  12.8 us

profile of v1, /device:TPU:1, one launch (start us, length us, event | category | flops | bytes accessed | tf_op | source)
XLA Modules:
  0.0 96.2 jit_solution(9855904223915800658)
XLA Ops:
  0.7 0.7 fusion.4
  1.4 0.8 and_select_fusion.8
  2.1 0.2 convert_reduce_fusion
  2.3 0.1 select_reduce_fusion
  2.4 0.8 fusion.2
  3.2 0.7 fusion.3
  3.9 0.6 stack.2.table
  4.5 1.6 %convert_element_type.7.rounded = bf16[2,256,128]{2,1,0:T(8,128)(2,1)} convert(f32[2,256,128]{2,1,0:T(8,128)} %panels.1) | non-fusion elementwise | flops 65536 | bytes 393216 | tf_op jit(solution)/shard_map/convert_element_type | solution.py:426
  6.2 43.0 %field.1 = (f32[2,256,128]{2,1,0:T(8,128)}, f32[32,4,128]{2,1,0:T(4,128)}) custom-call(s32[5,48]{1,0:T(8,128)} %stack.2.table, f32[2,256,128]{2,1,0:T(8,128)} %panels.1, bf16[2,256,128]{2,1,0:T(8,128)(2,1)} %convert_element_type.7.rounded, bf16[48,512,256]{2,1,0:T(8,128)(2,1)} %blocks_hbm.1), custom_call_target="tpu_custom_call" | custom-call | tf_op jit(solution)/shard_map/field/pallas_call | solution.py:224
  49.2 34.2 %sum_gram.1.gram = f32[128,128]{1,0:T(8,128)} custom-call(f32[32,4,128]{2,1,0:T(4,128)} %get-tuple-element.7.gram), custom_call_target="tpu_custom_call" | custom-call | tf_op jit(solution)/shard_map/sum_gram/pallas_call | solution.py:369
  83.4 12.8 %basis.1 = f32[2,256,128]{2,1,0:T(8,128)} custom-call(f32[128,128]{1,0:T(8,128)} %sum_gram.1.gram, f32[2,256,128]{2,1,0:T(8,128)} %get-tuple-element.8.field), custom_call_target="tpu_custom_call" | custom-call | tf_op jit(solution)/shard_map/basis/pallas_call | solution.py:430
  (2 shorter events, 0.0 us)

commit v2 on v1

v2 whole, which is shorter than its diff:
```python
import functools

import jax
import jax.numpy as jnp
from jax import lax
from jax.experimental import pallas as pl
from jax.experimental.pallas import tpu as pltpu
from jax.sharding import PartitionSpec as P

MESH = pl.DeviceIdType.MESH
BAND = 8
SIDE = 4
PLANE = SIDE * SIDE
PIVOTS = 4
RELAY_MIDDLE = 1
RELAY_LAST = 5
CHUNKS = 8
VMEM_LIMIT = 60 * 1024 * 1024


def remote(src, dst, send_sem, recv_sem, img, rep):
    return pltpu.make_async_remote_copy(
        src_ref=src,
        dst_ref=dst,
        send_sem=send_sem,
        recv_sem=recv_sem,
        device_id=(img, rep),
        device_id_type=MESH,
    )


def pair_tables(pairs, counts):
    slots = pairs.shape[0]
    capacity = slots // BAND
    devices = lax.axis_size("img")
    own = lax.axis_index("img")
    ids = jnp.arange(slots, dtype=jnp.int32)
    alive = ids < counts[0]
    first = pairs[:, 0] & 1
    second = pairs[:, 1] & 1
    offset = (pairs[:, 1] // 2 - own - 1) % devices
    same = (offset[:, None] == offset[None, :]) & (ids[None, :] < ids[:, None])
    rank = jnp.sum((same & alive[None, :]).astype(jnp.int32), axis=1)
    target = jnp.where(alive, offset * capacity + rank, slots)
    code = ids * 8 + first * 2 + second
    hit = target[None, :] == ids[:, None]
    empty = 2 * 2
    placed = empty + jnp.sum(jnp.where(hit, code - empty, 0), axis=1)
    far = offset * 2 + second
    far_0 = jnp.where(alive & (first == 0), far, 2 * BAND + 2)
    far_1 = jnp.where(alive & (first == 1), far, 2 * BAND + 2)
    return jnp.stack([placed // 8, (placed // 2) % 4, placed % 2, far_0, far_1])


def each(first, last, act):
    def body(t, _):
        act(t)
        return 0

    lax.fori_loop(first, last, body, 0)


def field_kernel(
    table,
    panels,
    blocks_hbm,
    field,
    gram,
    blocks,
    far,
    near_other,
    near,
    turned,
    returned,
    sums,
    raised,
    lifted,
    part,
    part_other,
    local,
    corner_parts,
    column,
    levels,
    pieces,
    load_sem,
    far_send,
    far_recv,
    near_send,
    near_recv,
    back_send,
    back_recv,
    up_send,
    up_recv,
    part_send,
    part_recv,
    s1,
    r1,
    s2,
    r2,
    s3,
    r3,
    s4,
    r4,
):
    me = lax.axis_index("img")
    rep = lax.axis_index("rep")
    devices = lax.axis_size("img")
    slots, keypts, half = blocks.shape
    univ = panels.shape[2]
    capacity = slots // BAND
    step = slots // CHUNKS
    height = devices // PLANE
    z = me // PLANE
    x = (me // SIDE) % SIDE
    y = me % SIDE
    above = (me + SIDE) % devices
    below = (me + devices - SIDE) % devices
    own_row = 2 * BAND
    zero_row = 2 * BAND + 2

    def load(chunk):
        rows = pl.ds(chunk * step, step)
        return pltpu.make_async_copy(blocks_hbm.at[rows], blocks.at[rows], load_sem.at[chunk])

    for chunk in range(CHUNKS):
        load(chunk).start()

    rank = y * 2 + rep

    def in_corner(t):
        other = (rank + t) % (2 * SIDE)
        return other, me - y + other // 2, other % 2

    def in_column(t):
        other = (x + t) % SIDE
        return other, z * PLANE + other * SIDE + y

    def in_levels(t):
        return ((z + t) % height) * PLANE + me % PLANE

    barrier = pltpu.get_barrier_semaphore()

    def greet(img, core):
        pl.semaphore_signal(barrier, inc=1, device_id=(img, core), device_id_type=MESH)

    def greet_corner(t):
        _, img, core = in_corner(t)
        greet(img, core)

    each(1, height, lambda t: greet(in_levels(t), rep))
    each(1, 2 * SIDE, greet_corner)
    each(1, SIDE, lambda t: greet(in_column(t)[1], rep))
    greet(above, rep)
    greet(below, rep)

    here = pl.ds(pl.multiple_of(rep * half, half), half)
    there = pl.ds(pl.multiple_of((1 - rep) * half, half), half)
    for image in range(2):
        far[own_row + image] = panels[image].astype(far.dtype)
        near[image, :, here] = panels[image].T.astype(near.dtype)
    far[zero_row] = jnp.zeros((half, univ), far.dtype)
    near[2] = jnp.zeros((univ, keypts), near.dtype)

    pl.semaphore_wait(barrier, height - 1 + 2 * SIDE - 1 + SIDE - 1 + 2)

    def far_rows(slot):
        return far.at[pl.ds(2 * slot, 2)]

    def mate(dy):
        return me - y + (y + dy) % SIDE

    def down(source, slot, sem):
        return remote(far_rows(source), far_rows(slot), far_send.at[sem], far_recv.at[slot], below, rep)

    def side(source, slot, sem, dy):
        return remote(
            far_rows(source), far_rows(slot), far_send.at[sem], far_recv.at[slot], mate(dy), rep
        )

    def own_side(dy):
        return side(BAND, 3 - dy, 1 + dy, dy)

    def middle_side(dy):
        return side(3, jnp.where(y + dy < SIDE, 3 - dy, 7 - dy), 4 + dy, dy)

    def last_side(dy):
        return side(7, 7 - dy, 7 + dy, dy)

    near_copy = remote(
        far_rows(BAND), near_other, near_send, near_recv, me, 1 - rep
    )
    near_copy.start()
    first_down = down(BAND, 3, 0)
    second_down = down(3, 7, 1)
    first_down.start()
    for dy in range(1, SIDE):

        @pl.when(y + dy >= SIDE)
        def _():
            own_side(dy).start()

    near_copy.wait()
    for image in range(2):
        near[image, :, there] = near_other[image].astype(jnp.float32).T.astype(near.dtype)
    for chunk in range(CHUNKS):
        load(chunk).wait()

    def back_copy(k):
        return remote(
            turned.at[k - 1],
            returned.at[k - 1],
            back_send.at[k - 1],
            back_recv.at[k - 1],
            mate(k % SIDE),
            rep,
        )

    def reverse(t):
        k = BAND - t
        totals = [jnp.zeros((univ, half), jnp.float32) for _ in range(2)]
        for r in range(capacity):
            q = (k - 1) * capacity + r
            product = jnp.dot(
                near[table[1, q]], blocks[table[0, q]], preferred_element_type=jnp.float32
            )
            product = product.astype(jnp.bfloat16).astype(jnp.float32)
            share = table[2, q].astype(jnp.float32)
            totals[0] = totals[0] + product * (1.0 - share)
            totals[1] = totals[1] + product * share
        for image in range(2):
            turned[k - 1, image] = totals[image].T.astype(turned.dtype)

        @pl.when(k % SIDE != 0)
        def _():
            back_copy(k).start()

    def relay_middle():
        far_wait(3)
        second_down.start()
        for dy in range(1, SIDE):
            middle_side(dy).start()

    def relay_last():
        far_wait(7)
        for dy in range(1, SIDE):

            @pl.when(y + dy < SIDE)
            def _():
                last_side(dy).start()

    def far_wait(slot):
        remote(
            far_rows(slot), far_rows(slot), far_send.at[0], far_recv.at[slot], below, rep
        ).wait_recv()

    def reverse_and_relay(t):
        reverse(t)

        @pl.when(t == RELAY_MIDDLE)
        def _():
            relay_middle()

        @pl.when(t == RELAY_LAST)
        def _():
            relay_last()

    each(0, BAND, reverse_and_relay)

    def add(slot, source, k):
        for image in range(2):
            sums[slot, image] += source[k, image].astype(jnp.float32)

    def lift(slot, which):
        for image in range(2):
            raised[which, image] = sums[slot, image].astype(raised.dtype)
        return up(which)

    def up(which):
        return remote(
            raised.at[which], lifted.at[which], up_send.at[which], up_recv.at[which], above, rep
        )

    def back_wait(k):
        back_copy(k).wait_recv()

    for image in range(2):
        sums[0, image] = jnp.zeros((half, univ), jnp.float32)
        sums[1, image] = turned[3, image].astype(jnp.float32)
        sums[2, image] = turned[7, image].astype(jnp.float32)

    for dy in range(1, SIDE):
        back_wait(4 + dy)
        add(jnp.where(y >= dy, 1, 2), returned, 3 + dy)
    lift(2, 0).start()

    for slot in (0, 1, 2, 4, 5, 6):
        far_wait(slot)

    group = 8

    def forward(rows, out):
        out[...] = jnp.zeros_like(out)

        def one(g):
            left = []
            right = []
            for r in range(group):
                s = g * group + r
                left.append(blocks[s, rows, :])
                right.append(jnp.concatenate([far[table[3, s]], far[table[4, s]]], axis=1))
            out[...] += jnp.dot(
                jnp.concatenate(left, axis=1),
                jnp.concatenate(right, axis=0),
                preferred_element_type=jnp.float32,
            )

        each(0, slots // group, one)

    part_copy = remote(part.at[0], part_other, part_send, part_recv, me, 1 - rep)
    forward(there, part.at[0])
    part_copy.start()

    for dy in range(1, SIDE):
        back_wait(dy)
        add(jnp.where(y >= dy, 0, 1), returned, dy - 1)
    up(0).wait_recv()
    add(1, lifted, 0)
    lift(1, 1).start()

    forward(here, part.at[1])
    part_copy.wait_recv()
    up(1).wait_recv()

    total = jnp.zeros((univ, univ), jnp.float32)
    for image in range(2):
        columns = pl.ds(image * univ, univ)
        value = panels[image] + part[1, :, columns] + part_other[:, columns]
        value = value + sums[0, image] + lifted[1, image].astype(jnp.float32)
        field[image] = value
        total = total + lax.dot_general(
            value,
            value,
            (((0,), (0,)), ((), ())),
            precision=lax.Precision.HIGHEST,
            preferred_element_type=jnp.float32,
        )

    width = local.shape[1]
    for r in range(2 * SIDE):
        local[r] = total[r * width : (r + 1) * width]

    def scatter_corner(t):
        other, img, core = in_corner(t)
        return remote(local.at[other], corner_parts.at[t - 1], s1.at[t - 1], r1.at[t - 1], img, core)

    def along_column(t, source):
        _, img = in_column(t)
        return remote(column.at[source], column.at[source], s2.at[t - 1], r2.at[t - 1], img, rep)

    def across(t, source):
        return remote(
            levels.at[source], levels.at[source], s3.at[t - 1], r3.at[t - 1], in_levels(t), rep
        )

    def gather_corner(t, source):
        _, img, core = in_corner(t)
        return remote(
            pieces.at[source], pieces.at[source], s4.at[t - 1], r4.at[t - 1], img, core
        )

    each(1, 2 * SIDE, lambda t: scatter_corner(t).start())
    each(1, 2 * SIDE, lambda t: scatter_corner(t).wait_recv())
    line = local[rank]
    for t in range(2 * SIDE - 1):
        line = line + corner_parts[t]
    column[x] = line
    each(1, SIDE, lambda t: along_column(t, x).start())
    each(1, SIDE, lambda t: along_column(t, (x + SIDE - t) % SIDE).wait_recv())
    line = column[0]
    for t in range(1, SIDE):
        line = line + column[t]
    levels[z] = line
    each(1, height, lambda t: across(t, z).start())
    each(1, height, lambda t: across(t, (z + height - t) % height).wait_recv())
    line = levels[0]
    for t in range(1, height):
        line = line + levels[t]
    pieces[rank] = line
    each(1, 2 * SIDE, lambda t: gather_corner(t, rank).start())
    each(1, 2 * SIDE, lambda t: gather_corner(t, (rank + 2 * SIDE - t) % (2 * SIDE)).wait_recv())
    for r in range(2 * SIDE):
        gram[r * width : (r + 1) * width] = pieces[r]

    first_down.wait_send()
    second_down.wait_send()
    for dy in range(1, SIDE):
        middle_side(dy).wait_send()

        @pl.when(y + dy >= SIDE)
        def _():
            own_side(dy).wait_send()

        @pl.when(y + dy < SIDE)
        def _():
            last_side(dy).wait_send()

        back_copy(dy).wait_send()
        back_copy(4 + dy).wait_send()
    up(0).wait_send()
    up(1).wait_send()
    part_copy.wait_send()
    each(1, 2 * SIDE, lambda t: scatter_corner(t).wait_send())
    each(1, SIDE, lambda t: along_column(t, x).wait_send())
    each(1, height, lambda t: across(t, z).wait_send())
    each(1, 2 * SIDE, lambda t: gather_corner(t, rank).wait_send())


def field_and_gram(table, panels, blocks):
    slots, keypts, half = blocks.shape
    univ = panels.shape[2]
    height = lax.axis_size("img") // PLANE
    line = 2 * SIDE
    width = univ // line
    dma = pltpu.SemaphoreType.DMA
    return pl.pallas_call(
        field_kernel,
        out_shape=(
            jax.ShapeDtypeStruct(panels.shape, jnp.float32),
            jax.ShapeDtypeStruct((univ, univ), jnp.float32),
        ),
        in_specs=[
            pl.BlockSpec(memory_space=pltpu.SMEM),
            pl.BlockSpec(memory_space=pltpu.VMEM),
            pl.BlockSpec(memory_space=pl.ANY),
        ],
        out_specs=(
            pl.BlockSpec(memory_space=pltpu.VMEM),
            pl.BlockSpec(memory_space=pltpu.VMEM),
        ),
        scratch_shapes=[
            pltpu.VMEM((slots, keypts, half), jnp.bfloat16),
            pltpu.VMEM((2 * BAND + 3, half, univ), jnp.bfloat16),
            pltpu.VMEM((2, half, univ), jnp.bfloat16),
            pltpu.VMEM((3, univ, keypts), jnp.bfloat16),
            pltpu.VMEM((BAND, 2, half, univ), jnp.bfloat16),
            pltpu.VMEM((BAND - 1, 2, half, univ), jnp.bfloat16),
            pltpu.VMEM((3, 2, half, univ), jnp.float32),
            pltpu.VMEM((2, 2, half, univ), jnp.bfloat16),
            pltpu.VMEM((2, 2, half, univ), jnp.bfloat16),
            pltpu.VMEM((2, half, 2 * univ), jnp.float32),
            pltpu.VMEM((half, 2 * univ), jnp.float32),
            pltpu.VMEM((line, width, univ), jnp.float32),
            pltpu.VMEM((line - 1, width, univ), jnp.float32),
            pltpu.VMEM((SIDE, width, univ), jnp.float32),
            pltpu.VMEM((height, width, univ), jnp.float32),
            pltpu.VMEM((line, width, univ), jnp.float32),
            dma((CHUNKS,)),
            dma((11,)),
            dma((BAND,)),
            dma,
            dma,
            dma((BAND - 1,)),
            dma((BAND - 1,)),
            dma((2,)),
            dma((2,)),
            dma,
            dma,
        ]
        + [dma((n - 1,)) for n in (line, SIDE, height, line) for _ in range(2)],
        compiler_params=pltpu.CompilerParams(
            collective_id=0, has_side_effects=True, vmem_limit_bytes=VMEM_LIMIT
        ),
        name="field",
    )(table, panels, blocks)


def basis_kernel(scale, gram, field, basis):
    univ = gram.shape[0]
    left = gram[...] * scale
    rows = lax.broadcasted_iota(jnp.int32, (univ, univ), 0)
    columns = lax.broadcasted_iota(jnp.int32, (univ, univ), 1)
    right = (rows == columns).astype(jnp.float32)
    scales = jnp.zeros((univ, univ), jnp.float32)
    for j in range(0, univ, PIVOTS):
        top = (j // 8) * 8
        at = j - top
        low = left[top:]
        low_right = right[top:]
        low_rows = rows[top:]
        unit = [[None] * PIVOTS for _ in range(PIVOTS)]
        pivots = []
        inverses = []
        for t in range(PIVOTS):
            entry = [
                jnp.broadcast_to(low[at + a : at + a + 1, j + t : j + t + 1], (1, univ))
                for a in range(t, PIVOTS)
            ]
            for u in range(t):
                for a in range(t, PIVOTS):
                    entry[a - t] = entry[a - t] - unit[a][u] * (unit[t][u] * pivots[u])
            pivots.append(entry[0])
            inverses.append(1.0 / entry[0])
            for a in range(t + 1, PIVOTS):
                unit[a][t] = entry[a - t] * inverses[t]
        row = []
        row_right = []
        factor = []
        for t in range(PIVOTS):
            one = low[at + t : at + t + 1]
            one_right = low_right[at + t : at + t + 1]
            column = jnp.broadcast_to(low[:, j + t : j + t + 1], low.shape)
            for u in range(t):
                one = one - unit[t][u] * row[u]
                one_right = one_right - unit[t][u] * row_right[u]
                column = column - factor[u] * (unit[t][u] * pivots[u])
            row.append(one)
            row_right.append(one_right)
            factor.append(column * inverses[t])
        below = low_rows >= j + PIVOTS
        for t in range(PIVOTS):
            share = jnp.where(below, factor[t], 0.0)
            low = low - share * row[t]
            low_right = low_right - share * row_right[t]
            scales = jnp.where(rows == j + t, lax.rsqrt(pivots[t]), scales)
        for t in range(1, PIVOTS):
            low_right = jnp.where(low_rows == j + t, row_right[t], low_right)
        left = jnp.concatenate([left[:top], low], axis=0) if top else low
        right = jnp.concatenate([right[:top], low_right], axis=0) if top else low_right
    inverse_factor = right * scales
    for image in range(field.shape[0]):
        basis[image] = lax.dot_general(
            field[image],
            inverse_factor,
            (((1,), (1,)), ((), ())),
            precision=lax.Precision.HIGHEST,
            preferred_element_type=jnp.float32,
        )


def shards(panels, blocks, pairs, counts):
    table = pair_tables(pairs, counts)
    field, gram = field_and_gram(table, panels, blocks)
    rows = lax.axis_size("img") * panels.shape[0] * lax.axis_size("rep") * panels.shape[1]
    return pl.pallas_call(
        functools.partial(basis_kernel, 1.0 / rows),
        out_shape=jax.ShapeDtypeStruct(panels.shape, jnp.float32),
        in_specs=[pl.BlockSpec(memory_space=pltpu.VMEM)] * 2,
        out_specs=pl.BlockSpec(memory_space=pltpu.VMEM),
        name="basis",
    )(gram, field)


def solution(mesh):
    in_specs = (P("img", "rep", None), P("img", None, "rep"), P("img", None), P("img"))
    out_specs = P("img", "rep", None)
    return jax.shard_map(shards, mesh=mesh, in_specs=in_specs, out_specs=out_specs, check_vma=False)
```

time: 96.5 us -> 73.9 us (0.77)
  Pallas kernels: 90 us -> 69.1 us
  other arithmetic: 4.87 us -> 3.25 us
    pallas_call x1 -> x0, Pallas kernels: 34.2 us -> none  [summed_gram(): pl.pallas_call(sum_kernel, out_shape=jax.ShapeDtypeStruct((size * width,...]
    pallas_call x1, Pallas kernels: 43 us -> 62.6 us  [field_and_gram(): pl.pallas_call(field_kernel, out_shape=(jax.ShapeDtypeStruct(panels.shape...]
    pallas_call x1, Pallas kernels: 12.8 us -> 6.52 us  [shards(): pl.pallas_call(functools.partial(basis_kernel, 1.0 / rows), out_shape=jax...]
    convert_element_type x1 -> x0, other arithmetic: 1.62 us -> none  [shards(): rounded = panels.astype(jnp.bfloat16)]
where the time goes in v2:
time: 73.9 us; the launch traced here: 73.7 us
  Pallas kernels  69.1 us (94%)
  other arithmetic  3.25 us (4%)
    pallas_call x1, Pallas kernels, field_and_gram(): pl.pallas_call(field_kernel, out_shape=(jax.ShapeDtypeStruct(panels.shape...  62.6 us
    pallas_call x1, Pallas kernels, shards(): pl.pallas_call(functools.partial(basis_kernel, 1.0 / rows), out_shape=jax...  6.52 us

profile of v2, /device:TPU:1, one launch (start us, length us, event | category | flops | bytes accessed | tf_op | source)
XLA Modules:
  0.0 73.7 jit_solution(2251487075738007820)
XLA Ops:
  0.7 0.7 fusion.4
  1.4 0.8 %and_select_fusion.8 = (s32[48]{0:T(128)S(1)}, s32[48]{0:T(128)S(1)}) fusion(s32[]{:T(128)S(6)} %axis_index.15, s32[48,2]{0,1:T(2,128)} %param.6), kind=kLoop, calls=%fused_computation.26 | loop fusion | flops 1680 | bytes 772 | tf_op jit(solution)/shard_map/jit(remainder)/select_n | solution.py:41
  2.1 0.2 convert_reduce_fusion
  2.3 0.1 select_reduce_fusion
  2.4 0.8 %fusion.2 = (s32[1,48]{1,0:T(1,128)S(1)}, s32[1,48]{1,0:T(1,128)S(1)}, s32[1,48]{1,0:T(1,128)S(1)}, s32[1,48]{1,0:T(1,128)S(1)}, s32[1,48]{1,0:T(1,128)S(1)}) fusion(s32[]{:T(128)} %bitcast.66, s32[48,2]{0,1:T(2,128)} %param.6, s32[]{:T(128)S(6)} %axis_index.15, s32[48]{0:T(128)S(1)} %select_reduce_fusion), kind=kLoop, calls=%fused_computation.15 | loop fusion | flops 3696 | bytes 1544 | tf_op jit(solution)/shard_map/jit(_where)/select_n | solution.py:51
  3.2 0.7 fusion.3
  3.9 0.6 stack.2.table
  4.5 62.6 %field.1 = (f32[2,256,128]{2,1,0:T(8,128)}, f32[128,128]{1,0:T(8,128)}) custom-call(s32[5,48]{1,0:T(8,128)} %stack.2.table, f32[2,256,128]{2,1,0:T(8,128)} %panels.1, bf16[48,512,256]{2,1,0:T(8,128)(2,1)} %blocks_hbm.1), custom_call_target="tpu_custom_call" | custom-call | tf_op jit(solution)/shard_map/field/pallas_call | solution.py:425
  67.2 6.5 %basis.1 = f32[2,256,128]{2,1,0:T(8,128)} custom-call(f32[128,128]{1,0:T(8,128)} %get-tuple-element.7.gram, f32[2,256,128]{2,1,0:T(8,128)} %get-tuple-element.8.field), custom_call_target="tpu_custom_call" | custom-call | tf_op jit(solution)/shard_map/basis/pallas_call | solution.py:544
  (2 shorter events, 0.0 us)

commit v3 on v2

--- a/solution.py
+++ b/solution.py
@@ -12,8 +12,8 @@
 SIDE = 4
 PLANE = SIDE * SIDE
 PIVOTS = 4
-RELAY_MIDDLE = 1
-RELAY_LAST = 5
+EMPTY = 4
+ORDER = (6, 7, 5, 3, 1, 8, 2, 4)
 CHUNKS = 8
 VMEM_LIMIT = 60 * 1024 * 1024
 
@@ -29,27 +29,20 @@
     )
 
 
-def pair_tables(pairs, counts):
+def pair_codes(pairs, counts):
     slots = pairs.shape[0]
     capacity = slots // BAND
     devices = lax.axis_size("img")
     own = lax.axis_index("img")
     ids = jnp.arange(slots, dtype=jnp.int32)
     alive = ids < counts[0]
-    first = pairs[:, 0] & 1
-    second = pairs[:, 1] & 1
     offset = (pairs[:, 1] // 2 - own - 1) % devices
     same = (offset[:, None] == offset[None, :]) & (ids[None, :] < ids[:, None])
     rank = jnp.sum((same & alive[None, :]).astype(jnp.int32), axis=1)
     target = jnp.where(alive, offset * capacity + rank, slots)
-    code = ids * 8 + first * 2 + second
+    code = ids * 8 + (pairs[:, 0] & 1) * 2 + (pairs[:, 1] & 1)
     hit = target[None, :] == ids[:, None]
-    empty = 2 * 2
-    placed = empty + jnp.sum(jnp.where(hit, code - empty, 0), axis=1)
-    far = offset * 2 + second
-    far_0 = jnp.where(alive & (first == 0), far, 2 * BAND + 2)
-    far_1 = jnp.where(alive & (first == 1), far, 2 * BAND + 2)
-    return jnp.stack([placed // 8, (placed // 2) % 4, placed % 2, far_0, far_1])
+    return EMPTY + jnp.sum(jnp.where(hit, code[None, :] - EMPTY, 0), axis=1)
 
 
 def each(first, last, act):
@@ -61,13 +54,14 @@
 
 
 def field_kernel(
-    table,
+    codes,
     panels,
     blocks_hbm,
     field,
     gram,
     blocks,
     far,
+    beyond,
     near_other,
     near,
     turned,
@@ -115,8 +109,12 @@
     y = me % SIDE
     above = (me + SIDE) % devices
     below = (me + devices - SIDE) % devices
-    own_row = 2 * BAND
-    zero_row = 2 * BAND + 2
+    own_row = 2 * SIDE
+    zero_row = 2 * SIDE + 2
+
+    def read(q):
+        code = codes[q]
+        return code // 8, (code // 2) % 4, code % 2
 
     def load(chunk):
         rows = pl.ds(chunk * step, step)
@@ -159,45 +157,50 @@
         far[own_row + image] = panels[image].astype(far.dtype)
         near[image, :, here] = panels[image].T.astype(near.dtype)
     far[zero_row] = jnp.zeros((half, univ), far.dtype)
+    beyond[zero_row] = jnp.zeros((half, univ), far.dtype)
     near[2] = jnp.zeros((univ, keypts), near.dtype)
 
     pl.semaphore_wait(barrier, height - 1 + 2 * SIDE - 1 + SIDE - 1 + 2)
 
-    def far_rows(slot):
-        return far.at[pl.ds(2 * slot, 2)]
+    def rows_of(buffer, slot):
+        return buffer.at[pl.ds(2 * slot, 2)]
 
     def mate(dy):
         return me - y + (y + dy) % SIDE
 
-    def down(source, slot, sem):
-        return remote(far_rows(source), far_rows(slot), far_send.at[sem], far_recv.at[slot], below, rep)
-
-    def side(source, slot, sem, dy):
+    first_down = remote(
+        rows_of(far, SIDE), rows_of(far, SIDE - 1), far_send.at[0], far_recv.at[SIDE - 1], below, rep
+    )
+
+    def next_down(slot):
         return remote(
-            far_rows(source), far_rows(slot), far_send.at[sem], far_recv.at[slot], mate(dy), rep
-        )
-
-    def own_side(dy):
-        return side(BAND, 3 - dy, 1 + dy, dy)
-
-    def middle_side(dy):
-        return side(3, jnp.where(y + dy < SIDE, 3 - dy, 7 - dy), 4 + dy, dy)
-
-    def last_side(dy):
-        return side(7, 7 - dy, 7 + dy, dy)
-
-    near_copy = remote(
-        far_rows(BAND), near_other, near_send, near_recv, me, 1 - rep
-    )
+            rows_of(far, slot),
+            rows_of(beyond, slot),
+            far_send.at[1 + slot],
+            far_recv.at[SIDE + slot],
+            below,
+            rep,
+        )
+
+    def side(source, dy):
+        slot = SIDE - 1 - dy
+        return remote(
+            rows_of(far, source),
+            rows_of(far, slot),
+            far_send.at[SIDE + dy],
+            far_recv.at[slot],
+            mate(dy),
+            rep,
+        )
+
+    near_copy = remote(rows_of(far, SIDE), near_other, near_send, near_recv, me, 1 - rep)
     near_copy.start()
-    first_down = down(BAND, 3, 0)
-    second_down = down(3, 7, 1)
     first_down.start()
     for dy in range(1, SIDE):
 
         @pl.when(y + dy >= SIDE)
         def _():
-            own_side(dy).start()
+            side(SIDE, dy).start()
 
     near_copy.wait()
     for image in range(2):
@@ -205,9 +208,9 @@
     for chunk in range(CHUNKS):
         load(chunk).wait()
 
-    def back_copy(k):
+    def back_copy(k, source):
         return remote(
-            turned.at[k - 1],
+            source,
             returned.at[k - 1],
             back_send.at[k - 1],
             back_recv.at[k - 1],
@@ -215,56 +218,60 @@
             rep,
         )
 
+    def up(which, source):
+        return remote(source, lifted.at[which], up_send.at[which], up_recv.at[which], above, rep)
+
     def reverse(t):
-        k = BAND - t
+        k = ORDER[-1]
+        for at in range(BAND - 1):
+            k = jnp.where(t == at, ORDER[at], k)
         totals = [jnp.zeros((univ, half), jnp.float32) for _ in range(2)]
         for r in range(capacity):
-            q = (k - 1) * capacity + r
-            product = jnp.dot(
-                near[table[1, q]], blocks[table[0, q]], preferred_element_type=jnp.float32
-            )
+            slot, first, second = read((k - 1) * capacity + r)
+            product = jnp.dot(near[first], blocks[slot], preferred_element_type=jnp.float32)
             product = product.astype(jnp.bfloat16).astype(jnp.float32)
-            share = table[2, q].astype(jnp.float32)
+            share = second.astype(jnp.float32)
             totals[0] = totals[0] + product * (1.0 - share)
             totals[1] = totals[1] + product * share
         for image in range(2):
             turned[k - 1, image] = totals[image].T.astype(turned.dtype)
 
-        @pl.when(k % SIDE != 0)
+        @pl.when(k % 2 == 1)
         def _():
-            back_copy(k).start()
-
-    def relay_middle():
-        far_wait(3)
-        second_down.start()
-        for dy in range(1, SIDE):
-            middle_side(dy).start()
-
-    def relay_last():
-        far_wait(7)
-        for dy in range(1, SIDE):
-
-            @pl.when(y + dy < SIDE)
-            def _():
-                last_side(dy).start()
+            back_copy(k, turned.at[k - 1]).start()
+
+        @pl.when(k == 6)
+        def _():
+            up(2, turned.at[k - 1]).start()
+
+    each(0, BAND, reverse)
 
     def far_wait(slot):
         remote(
-            far_rows(slot), far_rows(slot), far_send.at[0], far_recv.at[slot], below, rep
+            rows_of(far, SIDE - 1),
+            rows_of(far, SIDE - 1),
+            far_send.at[0],
+            far_recv.at[slot],
+            below,
+            rep,
         ).wait_recv()
 
-    def reverse_and_relay(t):
-        reverse(t)
-
-        @pl.when(t == RELAY_MIDDLE)
+    far_wait(SIDE - 1)
+    next_down(SIDE - 1).start()
+    for dy in range(1, SIDE):
+
+        @pl.when(y + dy < SIDE)
         def _():
-            relay_middle()
-
-        @pl.when(t == RELAY_LAST)
-        def _():
-            relay_last()
-
-    each(0, BAND, reverse_and_relay)
+            side(SIDE - 1, dy).start()
+
+    up(2, raised.at[2]).wait_recv()
+    for image in range(2):
+        value = turned[1, image].astype(jnp.float32) + lifted[2, image].astype(jnp.float32)
+        raised[2, image] = value.astype(raised.dtype)
+    back_copy(2, raised.at[2]).start()
+    for slot in range(SIDE - 2, -1, -1):
+        far_wait(slot)
+        next_down(slot).start()
 
     def add(slot, source, k):
         for image in range(2):
@@ -273,63 +280,69 @@
     def lift(slot, which):
         for image in range(2):
             raised[which, image] = sums[slot, image].astype(raised.dtype)
-        return up(which)
-
-    def up(which):
-        return remote(
-            raised.at[which], lifted.at[which], up_send.at[which], up_recv.at[which], above, rep
-        )
+        up(which, raised.at[which]).start()
 
     def back_wait(k):
-        back_copy(k).wait_recv()
+        back_copy(k, raised.at[2]).wait_recv()
 
     for image in range(2):
         sums[0, image] = jnp.zeros((half, univ), jnp.float32)
         sums[1, image] = turned[3, image].astype(jnp.float32)
         sums[2, image] = turned[7, image].astype(jnp.float32)
 
-    for dy in range(1, SIDE):
+    for dy in (1, 3):
         back_wait(4 + dy)
         add(jnp.where(y >= dy, 1, 2), returned, 3 + dy)
-    lift(2, 0).start()
-
-    for slot in (0, 1, 2, 4, 5, 6):
-        far_wait(slot)
+    lift(2, 0)
 
     group = 8
 
-    def forward(rows, out):
-        out[...] = jnp.zeros_like(out)
-
+    def forward(rows, out, panel_buffer, offset, first_group):
         def one(g):
             left = []
             right = []
             for r in range(group):
-                s = g * group + r
-                left.append(blocks[s, rows, :])
-                right.append(jnp.concatenate([far[table[3, s]], far[table[4, s]]], axis=1))
+                place = g * group + r
+                slot, first, second = read(offset * capacity + place)
+                row = (place // capacity) * 2 + second
+                left.append(blocks[slot, rows, :])
+                right.append(
+                    jnp.concatenate(
+                        [
+                            panel_buffer[jnp.where(first == image, row, zero_row)]
+                            for image in range(2)
+                        ],
+                        axis=1,
+                    )
+                )
             out[...] += jnp.dot(
                 jnp.concatenate(left, axis=1),
                 jnp.concatenate(right, axis=0),
                 preferred_element_type=jnp.float32,
             )
 
-        each(0, slots // group, one)
+        if first_group:
+            out[...] = jnp.zeros_like(out)
+        each(0, SIDE * capacity // group, one)
 
     part_copy = remote(part.at[0], part_other, part_send, part_recv, me, 1 - rep)
-    forward(there, part.at[0])
-    part_copy.start()
+    forward(there, part.at[0], far, 0, True)
+    forward(here, part.at[1], far, 0, True)
 
     for dy in range(1, SIDE):
         back_wait(dy)
         add(jnp.where(y >= dy, 0, 1), returned, dy - 1)
-    up(0).wait_recv()
+    up(0, raised.at[0]).wait_recv()
     add(1, lifted, 0)
-    lift(1, 1).start()
-
-    forward(here, part.at[1])
+    lift(1, 1)
+
+    for slot in range(SIDE, BAND):
+        far_wait(slot)
+    forward(there, part.at[0], beyond, SIDE, False)
+    part_copy.start()
+    forward(here, part.at[1], beyond, SIDE, False)
     part_copy.wait_recv()
-    up(1).wait_recv()
+    up(1, raised.at[1]).wait_recv()
 
     total = jnp.zeros((univ, univ), jnp.float32)
     for image in range(2):
@@ -392,22 +405,14 @@
         gram[r * width : (r + 1) * width] = pieces[r]
 
     first_down.wait_send()
-    second_down.wait_send()
+    for slot in range(SIDE):
+        next_down(slot).wait_send()
     for dy in range(1, SIDE):
-        middle_side(dy).wait_send()
-
-        @pl.when(y + dy >= SIDE)
-        def _():
-            own_side(dy).wait_send()
-
-        @pl.when(y + dy < SIDE)
-        def _():
-            last_side(dy).wait_send()
-
-        back_copy(dy).wait_send()
-        back_copy(4 + dy).wait_send()
-    up(0).wait_send()
-    up(1).wait_send()
+        side(SIDE - 1, dy).wait_send()
+    for k in (1, 2, 3, 5, 7):
+        back_copy(k, raised.at[2]).wait_send()
+    for which in range(3):
+        up(which, raised.at[which]).wait_send()
     part_copy.wait_send()
     each(1, 2 * SIDE, lambda t: scatter_corner(t).wait_send())
     each(1, SIDE, lambda t: along_column(t, x).wait_send())
@@ -415,7 +420,7 @@
     each(1, 2 * SIDE, lambda t: gather_corner(t, rank).wait_send())
 
 
-def field_and_gram(table, panels, blocks):
+def field_and_gram(codes, panels, blocks):
     slots, keypts, half = blocks.shape
     univ = panels.shape[2]
     height = lax.axis_size("img") // PLANE
@@ -439,14 +444,15 @@
         ),
         scratch_shapes=[
             pltpu.VMEM((slots, keypts, half), jnp.bfloat16),
-            pltpu.VMEM((2 * BAND + 3, half, univ), jnp.bfloat16),
+            pltpu.VMEM((2 * SIDE + 3, half, univ), jnp.bfloat16),
+            pltpu.VMEM((2 * SIDE + 3, half, univ), jnp.bfloat16),
             pltpu.VMEM((2, half, univ), jnp.bfloat16),
             pltpu.VMEM((3, univ, keypts), jnp.bfloat16),
             pltpu.VMEM((BAND, 2, half, univ), jnp.bfloat16),
             pltpu.VMEM((BAND - 1, 2, half, univ), jnp.bfloat16),
             pltpu.VMEM((3, 2, half, univ), jnp.float32),
-            pltpu.VMEM((2, 2, half, univ), jnp.bfloat16),
-            pltpu.VMEM((2, 2, half, univ), jnp.bfloat16),
+            pltpu.VMEM((3, 2, half, univ), jnp.bfloat16),
+            pltpu.VMEM((3, 2, half, univ), jnp.bfloat16),
             pltpu.VMEM((2, half, 2 * univ), jnp.float32),
             pltpu.VMEM((half, 2 * univ), jnp.float32),
             pltpu.VMEM((line, width, univ), jnp.float32),
@@ -455,14 +461,14 @@
             pltpu.VMEM((height, width, univ), jnp.float32),
             pltpu.VMEM((line, width, univ), jnp.float32),
             dma((CHUNKS,)),
-            dma((11,)),
+            dma((BAND,)),
             dma((BAND,)),
             dma,
             dma,
             dma((BAND - 1,)),
             dma((BAND - 1,)),
-            dma((2,)),
-            dma((2,)),
+            dma((3,)),
+            dma((3,)),
             dma,
             dma,
         ]
@@ -471,7 +477,7 @@
             collective_id=0, has_side_effects=True, vmem_limit_bytes=VMEM_LIMIT
         ),
         name="field",
-    )(table, panels, blocks)
+    )(codes, panels, blocks)
 
 
 def basis_kernel(scale, gram, field, basis):
@@ -538,8 +544,8 @@
 
 
 def shards(panels, blocks, pairs, counts):
-    table = pair_tables(pairs, counts)
-    field, gram = field_and_gram(table, panels, blocks)
+    codes = pair_codes(pairs, counts)
+    field, gram = field_and_gram(codes, panels, blocks)
     rows = lax.axis_size("img") * panels.shape[0] * lax.axis_size("rep") * panels.shape[1]
     return pl.pallas_call(
         functools.partial(basis_kernel, 1.0 / rows),

time: 73.9 us -> 66 us (0.89)
  Pallas kernels: 69.1 us -> 62.9 us
  other arithmetic: 3.25 us -> 2.31 us
    pallas_call x1, Pallas kernels: 62.6 us -> 56.4 us  [field_and_gram(): pl.pallas_call(field_kernel, out_shape=(jax.ShapeDtypeStruct(panels.shape...]
    select_n x4 -> x2, other arithmetic: 2.26 us -> 0.79 us  [the longest x1 0.78 us: pair_codes(): offset = (pairs[:, 1] // 2 - own - 1) % devices]
where the time goes in v3:
time: 66 us; the launch traced here: 65.9 us
  Pallas kernels  62.9 us (95%)
  other arithmetic  2.31 us (4%)
  between operations  0.67 us (1%)
    pallas_call x1, Pallas kernels, field_and_gram(): pl.pallas_call(field_kernel, out_shape=(jax.ShapeDtypeStruct(panels.shape...  56.4 us
    pallas_call x1, Pallas kernels, shards(): pl.pallas_call(functools.partial(basis_kernel, 1.0 / rows), out_shape=jax...  6.52 us

profile of v3, /device:TPU:1, one launch (start us, length us, event | category | flops | bytes accessed | tf_op | source)
XLA Modules:
  0.0 65.9 jit_solution(4575785110461630805)
XLA Ops:
  0.7 0.7 %fusion.2 = s32[48]{0:T(128)S(1)} fusion(s32[]{:T(128)S(6)} %axis_index.15, s32[48,2]{0,1:T(2,128)} %param.6), kind=kLoop, calls=%fused_computation.20 | loop fusion | flops 1344 | bytes 388 | tf_op jit(solution)/shard_map/eq | solution.py:40
  1.4 0.8 %and_select_fusion.2 = (s32[48]{0:T(128)S(1)}, s32[48]{0:T(128)S(1)}) fusion(s32[]{:T(128)S(6)} %axis_index.15, s32[48,2]{0,1:T(2,128)} %param.6), kind=kLoop, calls=%fused_computation.12 | loop fusion | flops 1680 | bytes 772 | tf_op jit(solution)/shard_map/jit(remainder)/select_n | solution.py:39
  2.1 0.2 convert_reduce_fusion
  2.3 0.1 select_reduce_fusion
  2.4 0.5 broadcast_add_fusion.codes
  3.0 56.4 %field.1 = (f32[2,256,128]{2,1,0:T(8,128)}, f32[128,128]{1,0:T(8,128)}) custom-call(s32[48]{0:T(128)} %broadcast_add_fusion.codes, f32[2,256,128]{2,1,0:T(8,128)} %panels.1, bf16[48,512,256]{2,1,0:T(8,128)(2,1)} %blocks_hbm.1), custom_call_target="tpu_custom_call" | custom-call | tf_op jit(solution)/shard_map/field/pallas_call | solution.py:430
  59.4 6.5 %basis.1 = f32[2,256,128]{2,1,0:T(8,128)} custom-call(f32[128,128]{1,0:T(8,128)} %get-tuple-element.7.gram, f32[2,256,128]{2,1,0:T(8,128)} %get-tuple-element.8.field), custom_call_target="tpu_custom_call" | custom-call | tf_op jit(solution)/shard_map/basis/pallas_call | solution.py:550
  (2 shorter events, 0.0 us)

commit v4 on v3

--- a/solution.py
+++ b/solution.py
@@ -13,6 +13,7 @@
 PLANE = SIDE * SIDE
 PIVOTS = 4
 EMPTY = 4
+LANES = 128
 ORDER = (6, 7, 5, 3, 1, 8, 2, 4)
 CHUNKS = 8
 VMEM_LIMIT = 60 * 1024 * 1024
@@ -29,20 +30,22 @@
     )
 
 
-def pair_codes(pairs, counts):
-    slots = pairs.shape[0]
-    capacity = slots // BAND
-    devices = lax.axis_size("img")
-    own = lax.axis_index("img")
-    ids = jnp.arange(slots, dtype=jnp.int32)
-    alive = ids < counts[0]
-    offset = (pairs[:, 1] // 2 - own - 1) % devices
-    same = (offset[:, None] == offset[None, :]) & (ids[None, :] < ids[:, None])
-    rank = jnp.sum((same & alive[None, :]).astype(jnp.int32), axis=1)
-    target = jnp.where(alive, offset * capacity + rank, slots)
-    code = ids * 8 + (pairs[:, 0] & 1) * 2 + (pairs[:, 1] & 1)
-    hit = target[None, :] == ids[:, None]
-    return EMPTY + jnp.sum(jnp.where(hit, code[None, :] - EMPTY, 0), axis=1)
+def pair_codes(pairs, scratch, live, own, devices, capacity):
+    lanes = scratch.shape[1]
+    slots = pairs.shape[1]
+    scratch[...] = jnp.zeros_like(scratch)
+    scratch[0:2, 0:slots] = pairs[...]
+    first = scratch[0:1, :]
+    second = scratch[1:2, :]
+    across = lax.broadcasted_iota(jnp.int32, (lanes, lanes), 1)
+    down = lax.broadcasted_iota(jnp.int32, (lanes, lanes), 0)
+    offset = jnp.broadcast_to(((second >> 1) - own - 1) & (devices - 1), (lanes, lanes))
+    before = (offset.T == offset) & (down < across) & (down < live)
+    rank = jnp.sum(jnp.where(before, 1, 0), axis=0, keepdims=True)
+    code = across * 8 + (first & 1) * 2 + (second & 1)
+    target = jnp.where(across < live, offset * capacity + rank, lanes)
+    hit = target.T == across
+    return EMPTY + jnp.sum(jnp.where(hit, code.T - EMPTY, 0), axis=0, keepdims=True)
 
 
 def each(first, last, act):
@@ -54,11 +57,15 @@
 
 
 def field_kernel(
-    codes,
+    counts,
+    pairs,
     panels,
     blocks_hbm,
     field,
     gram,
+    codes,
+    code_row,
+    pair_rows,
     blocks,
     far,
     beyond,
@@ -77,6 +84,7 @@
     levels,
     pieces,
     load_sem,
+    code_sem,
     far_send,
     far_recv,
     near_send,
@@ -113,7 +121,7 @@
     zero_row = 2 * SIDE + 2
 
     def read(q):
-        code = codes[q]
+        code = codes[0, q]
         return code // 8, (code // 2) % 4, code % 2
 
     def load(chunk):
@@ -150,6 +158,10 @@
     each(1, SIDE, lambda t: greet(in_column(t)[1], rep))
     greet(above, rep)
     greet(below, rep)
+
+    code_row[...] = pair_codes(pairs, pair_rows, counts[0], me, devices, capacity)
+    code_copy = pltpu.make_async_copy(code_row, codes, code_sem)
+    code_copy.start()
 
     here = pl.ds(pl.multiple_of(rep * half, half), half)
     there = pl.ds(pl.multiple_of((1 - rep) * half, half), half)
@@ -203,6 +215,7 @@
             side(SIDE, dy).start()
 
     near_copy.wait()
+    code_copy.wait()
     for image in range(2):
         near[image, :, there] = near_other[image].astype(jnp.float32).T.astype(near.dtype)
     for chunk in range(CHUNKS):
@@ -236,10 +249,6 @@
         for image in range(2):
             turned[k - 1, image] = totals[image].T.astype(turned.dtype)
 
-        @pl.when(k % 2 == 1)
-        def _():
-            back_copy(k, turned.at[k - 1]).start()
-
         @pl.when(k == 6)
         def _():
             up(2, turned.at[k - 1]).start()
@@ -264,6 +273,8 @@
         def _():
             side(SIDE - 1, dy).start()
 
+    for k in (7, 5, 3, 1):
+        back_copy(k, turned.at[k - 1]).start()
     up(2, raised.at[2]).wait_recv()
     for image in range(2):
         value = turned[1, image].astype(jnp.float32) + lifted[2, image].astype(jnp.float32)
@@ -290,7 +301,7 @@
         sums[1, image] = turned[3, image].astype(jnp.float32)
         sums[2, image] = turned[7, image].astype(jnp.float32)
 
-    for dy in (1, 3):
+    for dy in (3, 1):
         back_wait(4 + dy)
         add(jnp.where(y >= dy, 1, 2), returned, 3 + dy)
     lift(2, 0)
@@ -420,7 +431,7 @@
     each(1, 2 * SIDE, lambda t: gather_corner(t, rank).wait_send())
 
 
-def field_and_gram(codes, panels, blocks):
+def field_and_gram(counts, pairs, panels, blocks):
     slots, keypts, half = blocks.shape
     univ = panels.shape[2]
     height = lax.axis_size("img") // PLANE
@@ -436,6 +447,7 @@
         in_specs=[
             pl.BlockSpec(memory_space=pltpu.SMEM),
             pl.BlockSpec(memory_space=pltpu.VMEM),
+            pl.BlockSpec(memory_space=pltpu.VMEM),
             pl.BlockSpec(memory_space=pl.ANY),
         ],
         out_specs=(
@@ -443,6 +455,9 @@
             pl.BlockSpec(memory_space=pltpu.VMEM),
         ),
         scratch_shapes=[
+            pltpu.SMEM((1, LANES), jnp.int32),
+            pltpu.VMEM((1, LANES), jnp.int32),
+            pltpu.VMEM((8, LANES), jnp.int32),
             pltpu.VMEM((slots, keypts, half), jnp.bfloat16),
             pltpu.VMEM((2 * SIDE + 3, half, univ), jnp.bfloat16),
             pltpu.VMEM((2 * SIDE + 3, half, univ), jnp.bfloat16),
@@ -461,6 +476,7 @@
             pltpu.VMEM((height, width, univ), jnp.float32),
             pltpu.VMEM((line, width, univ), jnp.float32),
             dma((CHUNKS,)),
+            dma,
             dma((BAND,)),
             dma((BAND,)),
             dma,
@@ -477,7 +493,7 @@
             collective_id=0, has_side_effects=True, vmem_limit_bytes=VMEM_LIMIT
         ),
         name="field",
-    )(codes, panels, blocks)
+    )(counts, pairs, panels, blocks)
 
 
 def basis_kernel(scale, gram, field, basis):
@@ -544,8 +560,7 @@
 
 
 def shards(panels, blocks, pairs, counts):
-    codes = pair_codes(pairs, counts)
-    field, gram = field_and_gram(codes, panels, blocks)
+    field, gram = field_and_gram(counts, pairs.T, panels, blocks)
     rows = lax.axis_size("img") * panels.shape[0] * lax.axis_size("rep") * panels.shape[1]
     return pl.pallas_call(
         functools.partial(basis_kernel, 1.0 / rows),

time: 66 us -> 61.6 us (0.933)
  other arithmetic: 2.31 us -> 0 us
  Pallas kernels: 62.9 us -> 60.8 us
    pallas_call x1, Pallas kernels: 56.4 us -> 54.3 us  [field_and_gram(): pl.pallas_call(field_kernel, out_shape=(jax.ShapeDtypeStruct(panels.shape...]
    select_n x2 -> x0, other arithmetic: 0.79 us -> none  [the longest x1 0.78 us: pair_codes(): offset = (pairs[:, 1] // 2 - own - 1) % devices]
    eq x1 -> x0, other arithmetic: 0.7 us -> none  [pair_codes(): same = (offset[:, None] == offset[None, :]) & (ids[None, :] < ids[:, None])]
where the time goes in v4:
time: 61.6 us; the launch traced here: 61.5 us
  Pallas kernels  60.8 us (99%)
  between operations  0.66 us (1%)
    pallas_call x1, Pallas kernels, field_and_gram(): pl.pallas_call(field_kernel, out_shape=(jax.ShapeDtypeStruct(panels.shape...  54.3 us
    pallas_call x1, Pallas kernels, shards(): pl.pallas_call(functools.partial(basis_kernel, 1.0 / rows), out_shape=jax...  6.52 us

profile of v4, /device:TPU:1, one launch (start us, length us, event | category | flops | bytes accessed | tf_op | source)
XLA Modules:
  0.0 61.5 jit_solution(3742328715581303492)
XLA Ops:
  0.7 54.3 %field.1 = (f32[2,256,128]{2,1,0:T(8,128)}, f32[128,128]{1,0:T(8,128)}) custom-call(s32[1]{0:T(128)S(6)} %copy.5.counts, s32[2,48]{1,0:T(2,128)} %bitcast.1, f32[2,256,128]{2,1,0:T(8,128)} %panels.1, bf16[48,512,256]{2,1,0:T(8,128)(2,1)} %blocks_hbm.1), custom_call_target="tpu_custom_call" | custom-call | tf_op jit(solution)/shard_map/field/pallas_call | solution.py:441
  55.0 6.5 %basis.1 = f32[2,256,128]{2,1,0:T(8,128)} custom-call(f32[128,128]{1,0:T(8,128)} %get-tuple-element.7.gram, f32[2,256,128]{2,1,0:T(8,128)} %get-tuple-element.8.field), custom_call_target="tpu_custom_call" | custom-call | tf_op jit(solution)/shard_map/basis/pallas_call | solution.py:565

commit v5 on v4

--- a/solution.py
+++ b/solution.py
@@ -14,7 +14,7 @@
 PIVOTS = 4
 EMPTY = 4
 LANES = 128
-ORDER = (6, 7, 5, 3, 1, 8, 2, 4)
+ORDER = (6, 7, 5, 8, 3, 1, 2, 4)
 CHUNKS = 8
 VMEM_LIMIT = 60 * 1024 * 1024
 
@@ -180,39 +180,47 @@
     def mate(dy):
         return me - y + (y + dy) % SIDE
 
-    first_down = remote(
-        rows_of(far, SIDE), rows_of(far, SIDE - 1), far_send.at[0], far_recv.at[SIDE - 1], below, rep
-    )
-
-    def next_down(slot):
+    def first_down(image):
         return remote(
-            rows_of(far, slot),
-            rows_of(beyond, slot),
-            far_send.at[1 + slot],
-            far_recv.at[SIDE + slot],
+            far.at[own_row + image],
+            far.at[2 * SIDE - 2 + image],
+            far_send.at[image],
+            far_recv.at[2 * SIDE - 2 + image],
             below,
             rep,
         )
 
-    def side(source, dy):
+    def next_down(slot, image):
+        return remote(
+            far.at[2 * slot + image],
+            beyond.at[2 * slot + image],
+            far_send.at[2 + 2 * slot + image],
+            far_recv.at[2 * SIDE + 2 * slot + image],
+            below,
+            rep,
+        )
+
+    def side(source, dy, image):
         slot = SIDE - 1 - dy
         return remote(
-            rows_of(far, source),
-            rows_of(far, slot),
-            far_send.at[SIDE + dy],
-            far_recv.at[slot],
+            far.at[2 * source + image],
+            far.at[2 * slot + image],
+            far_send.at[2 * SIDE + 2 * dy + image],
+            far_recv.at[2 * slot + image],
             mate(dy),
             rep,
         )
 
     near_copy = remote(rows_of(far, SIDE), near_other, near_send, near_recv, me, 1 - rep)
     near_copy.start()
-    first_down.start()
-    for dy in range(1, SIDE):
-
-        @pl.when(y + dy >= SIDE)
-        def _():
-            side(SIDE, dy).start()
+    for image in range(2):
+        first_down(image).start()
+    for image in range(2):
+        for dy in range(1, SIDE):
+
+            @pl.when(y + dy >= SIDE)
+            def _():
+                side(SIDE, dy, image).start()
 
     near_copy.wait()
     code_copy.wait()
@@ -253,27 +261,30 @@
         def _():
             up(2, turned.at[k - 1]).start()
 
-    each(0, BAND, reverse)
-
-    def far_wait(slot):
+    def far_wait(slot, image):
         remote(
-            rows_of(far, SIDE - 1),
-            rows_of(far, SIDE - 1),
+            far.at[2 * SIDE - 2],
+            far.at[2 * SIDE - 2],
             far_send.at[0],
-            far_recv.at[slot],
+            far_recv.at[2 * slot + image],
             below,
             rep,
         ).wait_recv()
 
-    far_wait(SIDE - 1)
-    next_down(SIDE - 1).start()
-    for dy in range(1, SIDE):
-
-        @pl.when(y + dy < SIDE)
-        def _():
-            side(SIDE - 1, dy).start()
-
-    for k in (7, 5, 3, 1):
+    each(0, BAND // 2, reverse)
+    for k in (7, 5):
+        back_copy(k, turned.at[k - 1]).start()
+    for image in range(2):
+        far_wait(SIDE - 1, image)
+        for dy in range(1, SIDE):
+
+            @pl.when(y + dy < SIDE)
+            def _():
+                side(SIDE - 1, dy, image).start()
+
+        next_down(SIDE - 1, image).start()
+    each(BAND // 2, BAND, reverse)
+    for k in (3, 1):
         back_copy(k, turned.at[k - 1]).start()
     up(2, raised.at[2]).wait_recv()
     for image in range(2):
@@ -281,8 +292,9 @@
         raised[2, image] = value.astype(raised.dtype)
     back_copy(2, raised.at[2]).start()
     for slot in range(SIDE - 2, -1, -1):
-        far_wait(slot)
-        next_down(slot).start()
+        for image in range(2):
+            far_wait(slot, image)
+            next_down(slot, image).start()
 
     def add(slot, source, k):
         for image in range(2):
@@ -348,7 +360,8 @@
     lift(1, 1)
 
     for slot in range(SIDE, BAND):
-        far_wait(slot)
+        for image in range(2):
+            far_wait(slot, image)
     forward(there, part.at[0], beyond, SIDE, False)
     part_copy.start()
     forward(here, part.at[1], beyond, SIDE, False)
@@ -415,11 +428,12 @@
     for r in range(2 * SIDE):
         gram[r * width : (r + 1) * width] = pieces[r]
 
-    first_down.wait_send()
-    for slot in range(SIDE):
-        next_down(slot).wait_send()
-    for dy in range(1, SIDE):
-        side(SIDE - 1, dy).wait_send()
+    for image in range(2):
+        first_down(image).wait_send()
+        for slot in range(SIDE):
+            next_down(slot, image).wait_send()
+        for dy in range(1, SIDE):
+            side(SIDE - 1, dy, image).wait_send()
     for k in (1, 2, 3, 5, 7):
         back_copy(k, raised.at[2]).wait_send()
     for which in range(3):
@@ -477,8 +491,8 @@
             pltpu.VMEM((line, width, univ), jnp.float32),
             dma((CHUNKS,)),
             dma,
-            dma((BAND,)),
-            dma((BAND,)),
+            dma((2 * BAND,)),
+            dma((2 * BAND,)),
             dma,
             dma,
             dma((BAND - 1,)),

time: 61.6 us -> 59.9 us (0.972)
  Pallas kernels: 60.8 us -> 59.1 us
    pallas_call x1, Pallas kernels: 54.3 us -> 52.6 us  [field_and_gram(): pl.pallas_call(field_kernel, out_shape=(jax.ShapeDtypeStruct(panels.shape...]
where the time goes in v5:
time: 59.9 us; the launch traced here: 59.8 us
  Pallas kernels  59.1 us (99%)
  between operations  0.66 us (1%)
    pallas_call x1, Pallas kernels, field_and_gram(): pl.pallas_call(field_kernel, out_shape=(jax.ShapeDtypeStruct(panels.shape...  52.6 us
    pallas_call x1, Pallas kernels, shards(): pl.pallas_call(functools.partial(basis_kernel, 1.0 / rows), out_shape=jax...  6.52 us

profile of v5, /device:TPU:1, one launch (start us, length us, event | category | flops | bytes accessed | tf_op | source)
XLA Modules:
  0.0 59.8 jit_solution(5960620035282880420)
XLA Ops:
  0.7 52.6 %field.1 = (f32[2,256,128]{2,1,0:T(8,128)}, f32[128,128]{1,0:T(8,128)}) custom-call(s32[1]{0:T(128)S(6)} %copy.5.counts, s32[2,48]{1,0:T(2,128)} %bitcast.1, f32[2,256,128]{2,1,0:T(8,128)} %panels.1, bf16[48,512,256]{2,1,0:T(8,128)(2,1)} %blocks_hbm.1), custom_call_target="tpu_custom_call" | custom-call | tf_op jit(solution)/shard_map/field/pallas_call | solution.py:455
  53.2 6.5 %basis.1 = f32[2,256,128]{2,1,0:T(8,128)} custom-call(f32[128,128]{1,0:T(8,128)} %get-tuple-element.7.gram, f32[2,256,128]{2,1,0:T(8,128)} %get-tuple-element.8.field), custom_call_target="tpu_custom_call" | custom-call | tf_op jit(solution)/shard_map/basis/pallas_call | solution.py:579
